TPU v7x, 32 devices: a whole 2x2x4 slice. The times are simulated.
32 devices in a mesh: groups: 2 (over y), space: 4 (over x, core), frame: 4 (over z).
Axes of the slice: x: 2, y: 2, z: 4, core: 2. Of those that a mesh axis runs over, the one named last changes fastest.
Arguments:
- clip: bfloat16 [8, 24, 32, 512], P(('groups', 'frame'), 'space'), parts along dimension 0, may hold values from -6 to 6
- cotangent: bfloat16 [8, 24, 32, 512], P(('groups', 'frame'), 'space'), parts along dimension 0, may hold values from -6 to 6
- tile_rows: int32 [8], P('groups'), parts along dimension 0, may hold values from 1 to 6, 12 in all
- frame_start: int32 [8, 32], P('groups'), parts along dimension 0, may hold values from 0 to 3, as said below
- norm_gain: float32 [512], replicated, may hold values from 0.1 to 1.9
- w_spatial: bfloat16 [9, 512, 512], P(None, 'space'), may hold values from -0.09375 to 0.09375
- w_temporal: bfloat16 [3, 512, 512], P(None, 'space'), may hold values from -0.15625 to 0.15625
- w_attn: bfloat16 [4, 512, 512], P(None, 'space'), may hold values from -0.25 to 0.25
Outputs:
- block_output: bfloat16 [8, 24, 32, 512], P(('groups', 'frame'), 'space'), parts along dimension 0
- clip_grad: bfloat16 [8, 24, 32, 512], P(('groups', 'frame'), 'space'), parts along dimension 0
There are 2 independent parts, one for each index of `groups`. A program takes and returns all parts, laid end to end along the dimension named above; an argument that names none is the same for every part. Nothing has to cross between parts.
Inputs may be any that keep to these rules, and one draw needn't show every extreme that they name: tile_rows[t] counts the frame rows of tile t, tiles in order down the frame; they sum to 12 and the largest is 6. frame_start[f,j] <= f for every frame f and column j; column 0 of the last frame starts at 3.
All inputs are finite; a program needn't handle non-finite values.
Results may differ from a plain program's by a relative error of at most 0.014.
Values may be sent and summed in bfloat16 or wider, within the bound.
A program may use at most 64 MiB of HBM per device.

v0:
```python
import jax
import jax.numpy as jnp
from jax import lax
from jax.sharding import PartitionSpec as P

NORM_EPSILON = 1e-06


def passed_along(value, axis, steps):
    count = lax.axis_size(axis)
    first, last = (max(0, -steps), min(count, count - steps))
    return lax.ppermute(value, axis, [(source, source + steps) for source in range(first, last)])


def tile_rim(edge_row, offset):
    return passed_along(edge_row, "space", offset)


def frame_rim(values, offset):
    return passed_along(values, "frame", offset)


def with_faces(values, row_count):
    height = values.shape[0]
    lowest = lax.dynamic_index_in_dim(values, row_count - 1, 0, keepdims=False)
    upper_face = tile_rim(lowest, 1)
    lower_face = tile_rim(values[0], -1)
    extended = jnp.concatenate([upper_face[None], values, jnp.zeros_like(values[:1])], 0)
    position = lax.broadcasted_iota(jnp.int32, (height + 2, 1, 1), 0)
    extended = jnp.where(position == row_count + 1, lower_face[None], extended)
    return jnp.pad(extended, ((0, 0), (1, 1), (0, 0)))


def spatial_conv(extended, kernel, flipped):
    height = extended.shape[0] - 2
    breadth = extended.shape[1] - 2
    summed = None
    for tap_row in range(3):
        for tap_col in range(3):
            patches = extended[tap_row : tap_row + height, tap_col : tap_col + breadth]
            if flipped:
                product = jnp.einsum(
                    "hwd,ed->hwe",
                    patches,
                    kernel[(2 - tap_row) * 3 + 2 - tap_col],
                    preferred_element_type=jnp.float32,
                )
            else:
                product = jnp.einsum(
                    "hwd,de->hwe",
                    patches,
                    kernel[tap_row * 3 + tap_col],
                    preferred_element_type=jnp.float32,
                )
            summed = product if summed is None else summed + product
    return summed


def project(values, matrix):
    return jnp.einsum("hwd,de->hwe", values, matrix, preferred_element_type=jnp.float32)


def project_back(values, matrix):
    return jnp.einsum("hwe,de->hwd", values, matrix, preferred_element_type=jnp.float32)


def per_device(clip, cotangent, tile_rows, frame_start, norm_gain, w_spatial, w_temporal, w_attn):
    height = clip.shape[1]
    breadth = clip.shape[2]
    channels = clip.shape[3]
    frames = lax.axis_size("frame")
    frame_now = lax.axis_index("frame")
    row_count = tile_rows[lax.axis_index("space")]
    live = (lax.broadcasted_iota(jnp.int32, (height, 1, 1), 0) < row_count).astype(jnp.float32)
    score_scale = channels ** (-0.5)
    kernel, temporal, attention = (
        lax.all_gather(w_spatial, "space", axis=1, tiled=True),
        lax.all_gather(w_temporal, "space", axis=1, tiled=True),
        lax.all_gather(w_attn, "space", axis=1, tiled=True),
    )
    inputs = clip[0].astype(jnp.float32)
    inverse = lax.rsqrt(jnp.mean(inputs * inputs, -1, keepdims=True) + NORM_EPSILON)
    normed = inputs * inverse
    hidden = (normed * norm_gain * live).astype(jnp.bfloat16)
    preact = spatial_conv(with_faces(hidden, row_count), kernel, False) * live
    activated = jax.nn.silu(preact).astype(jnp.bfloat16)
    mixed = (
        project(activated, temporal[0])
        + project(frame_rim(activated, 1), temporal[1])
        + project(frame_rim(activated, 2), temporal[2])
    )
    residual = ((inputs + mixed) * live).astype(jnp.bfloat16)
    queries = project(residual, attention[0]).astype(jnp.bfloat16)
    keys_own = project(residual, attention[1]).astype(jnp.bfloat16)
    values_own = project(residual, attention[2]).astype(jnp.bfloat16)
    upstream = cotangent[0].astype(jnp.float32) * live
    grad_out = upstream.astype(jnp.bfloat16)
    grad_attended = project_back(grad_out, attention[3]).astype(jnp.bfloat16)
    pixels = height * breadth
    share = pixels // frames
    outgoing = jnp.stack(
        [
            queries.reshape(1, pixels, channels),
            keys_own.reshape(1, pixels, channels),
            values_own.reshape(1, pixels, channels),
            grad_attended.reshape(1, pixels, channels),
        ]
    )
    arrived = lax.all_to_all(outgoing, "frame", split_axis=2, concat_axis=1, tiled=True)
    query_all = arrived[0]
    key_all = arrived[1]
    value_all = arrived[2]
    upward_all = arrived[3]
    frame_ids = lax.iota(jnp.int32, frames)
    columns = (frame_now * share + lax.iota(jnp.int32, share)) % breadth
    starts = jnp.take(frame_start, columns, axis=1)
    allowed = (frame_ids[None, :, None] >= starts[:, None, :]) & (
        frame_ids[None, :, None] <= frame_ids[:, None, None]
    )
    scores = (
        jnp.einsum("fpc,gpc->fgp", query_all, key_all, preferred_element_type=jnp.float32)
        * score_scale
    )
    scores = jnp.where(allowed, scores, -jnp.inf)
    probs = jax.nn.softmax(scores, axis=1)
    probs_low = probs.astype(jnp.bfloat16)
    attended_all = jnp.einsum(
        "fgp,gpc->fpc", probs_low, value_all, preferred_element_type=jnp.float32
    ).astype(jnp.bfloat16)
    grad_probs = jnp.einsum(
        "fpc,gpc->fgp", upward_all, value_all, preferred_element_type=jnp.float32
    )
    grad_scores = probs * (grad_probs - jnp.sum(probs * grad_probs, 1, keepdims=True))
    grad_scores_low = grad_scores.astype(jnp.bfloat16)
    grad_query_all = (
        jnp.einsum("fgp,gpc->fpc", grad_scores_low, key_all, preferred_element_type=jnp.float32)
        * score_scale
    ).astype(jnp.bfloat16)
    key_terms = (
        jnp.einsum("fgp,fpc->fgpc", grad_scores_low, query_all, preferred_element_type=jnp.float32)
        * score_scale
    ).astype(jnp.bfloat16)
    grad_key_all = jnp.sum(key_terms.astype(jnp.float32), 0).astype(jnp.bfloat16)
    value_terms = jnp.einsum(
        "fgp,fpc->fgpc", probs_low, upward_all, preferred_element_type=jnp.float32
    ).astype(jnp.bfloat16)
    grad_value_all = jnp.sum(value_terms.astype(jnp.float32), 0).astype(jnp.bfloat16)
    returning = jnp.stack([attended_all, grad_query_all, grad_key_all, grad_value_all])
    came_back = lax.all_to_all(returning, "frame", split_axis=1, concat_axis=2, tiled=True)
    attended = came_back[0, 0].reshape(height, breadth, channels)
    grad_queries = came_back[1, 0].reshape(height, breadth, channels)
    grad_keys_low = came_back[2, 0].reshape(height, breadth, channels)
    grad_values_low = came_back[3, 0].reshape(height, breadth, channels)
    block_output = ((residual.astype(jnp.float32) + project(attended, attention[3])) * live).astype(
        jnp.bfloat16
    )
    grad_resid = (
        upstream
        + project_back(grad_queries, attention[0])
        + project_back(grad_keys_low, attention[1])
        + project_back(grad_values_low, attention[2])
    )
    grad_resid = grad_resid * live
    grad_low = grad_resid.astype(jnp.bfloat16)
    grad_act = (
        project_back(grad_low, temporal[0])
        + project_back(frame_rim(grad_low, -1), temporal[1])
        + project_back(frame_rim(grad_low, -2), temporal[2])
    )
    sigmoid_pre = jax.nn.sigmoid(preact)
    grad_pre = (grad_act * sigmoid_pre * (1.0 + preact * (1.0 - sigmoid_pre)) * live).astype(
        jnp.bfloat16
    )
    grad_hidden = spatial_conv(with_faces(grad_pre, row_count), kernel, True)
    grad_normed = grad_hidden * norm_gain
    grad_inputs = inverse * (
        grad_normed - normed * jnp.mean(grad_normed * normed, -1, keepdims=True)
    )
    clip_grad = ((grad_resid + grad_inputs) * live).astype(jnp.bfloat16)
    return (block_output[None], clip_grad[None])


def solution(mesh):
    placed = (
        P(("groups", "frame"), "space", None, None),
        P(("groups", "frame"), "space", None, None),
        P("groups"),
        P("groups", None),
        P(),
        P(None, "space", None),
        P(None, "space", None),
        P(None, "space", None),
    )
    return jax.shard_map(
        per_device,
        mesh=mesh,
        in_specs=placed,
        out_specs=(
            P(("groups", "frame"), "space", None, None),
            P(("groups", "frame"), "space", None, None),
        ),
        check_vma=False,
    )
```

profile of v0, /device:TPU:1, one launch (start us, length us, event | category | flops | bytes accessed | tf_op | source)
XLA Modules:
  0.0 198.0 jit_solution(8891936423928351827)
XLA Ops:
  7.2 0.7 all-gather.8.cloned.1.call-update
  8.0 0.7 all-gather.4.cloned.1.call-update
  8.7 1.2 dynamic_slice.10
  11.3 0.6 compare_convert_fusion
  11.9 1.0 fusion.54
  13.0 1.1 fusion.47
  14.1 4.5 %collective-permute-start.1 = (bf16[32,512]{1,0:T(8,128)(2,1)S(1)}, bf16[32,512]{1,0:T(8,128)(2,1)S(1)}, u32[]{:S(2)}, u32[]{:S(2)}) collective-permute-start(bf16[32,512]{1,0:T(8,128)(2,1)S(1)} %get-tuple-element.15), channel_id=1, source_target_pairs={{0,4},{4,8},{8,12},{1,5},{5,9},{9,13},{2,6},{6,10},{10,14},{3,7},{... | collective-permute-start | bytes 98312 | tf_op jit(solution)/shard_map/ppermute | solution.py:12
  18.6 1.9 collective-permute-start
  21.3 3.8 %collective-permute-done = bf16[32,512]{1,0:T(8,128)(2,1)S(1)} collective-permute-done((bf16[32,512]{1,0:T(8,128)(2,1)S(1)}, bf16[32,512]{1,0:T(8,128)(2,1)S(1)}, u32[]{:S(2)}, u32[]{:S(2)}) %collective-permute-start) | collective-permute-done | bytes 32800 | tf_op jit(solution)/shard_map/ppermute | solution.py:12
  25.1 9.8 %all-gather.8.cloned.1.call-done = bf16[4,512,512]{2,1,0:T(8,128)(2,1)} async-done(((bf16[4,128,512]{2,1,0:T(8,128)(2,1)}), bf16[4,512,512]{2,1,0:T(8,128)(2,1)}) %all-gather.8.cloned.1.call-update) | async-done | bytes 2097168 | tf_op jit(solution)/shard_map/all_gather | solution.py:79
  35.0 1.4 convolution_convert_fusion.1
  36.3 0.3 copy.109
  36.6 37.3 %all-gather.4.cloned.1.call-done = bf16[9,512,512]{2,1,0:T(8,128)(2,1)} async-done(((bf16[9,128,512]{2,1,0:T(8,128)(2,1)}), bf16[9,512,512]{2,1,0:T(8,128)(2,1)}) %all-gather.4.cloned.1.call-update) | async-done | bytes 4718608 | tf_op jit(solution)/shard_map/all_gather | solution.py:77
  74.0 1.3 fusion.38
  75.3 1.3 fusion.39
  76.6 1.3 fusion.41
  77.9 1.3 fusion.35
  79.2 1.3 convolution_add_fusion.17
  80.5 1.3 convolution_add_fusion.16
  81.9 1.3 convolution_add_fusion.15
  83.2 1.3 fusion.10
  84.6 2.2 %multiply_convert_fusion.2 = (bf16[6,32,512]{2,1,0:T(8,128)(2,1)S(1)}, f32[6,32,512]{2,1,0:T(8,128)}) fusion(f32[6]{0:T(128)S(1)} %compare_convert_fusion, f32[6,32,512]{2,1,0:T(8,128)S(1)} %fusion.41, f32[6,32,512]{2,1,0:T(8,128)S(1)} %fusion.10, bf16[8,32,512]{2,1,0:T(8,128)(2,1)S(1)} %maximum_select_fusion, ...), kind=kOutput, calls=%fused_computation.104 | convolution fusion | flops 101449728 | bytes 2162712 | tf_op jit(solution)/shard_map/hwd,de->hwe/dot_general | solution.py:49
  86.8 3.1 %collective-permute-start.2 = (bf16[6,32,512]{2,1,0:T(8,128)(2,1)S(1)}, bf16[6,32,512]{2,1,0:T(8,128)(2,1)S(1)}, u32[]{:S(2)}, u32[]{:S(2)}) collective-permute-start(bf16[6,32,512]{2,1,0:T(8,128)(2,1)S(1)} %get-tuple-element.16), channel_id=1, source_target_pairs={{0,1},{1,2},{2,3},{4,5},{5,6},{6,7},{8,9},{9,10},{10,11},{12,13},{... | collective-permute-start | bytes 589832 | tf_op jit(solution)/shard_map/ppermute | solution.py:12
  89.9 4.0 %collective-permute-start.3 = (bf16[6,32,512]{2,1,0:T(8,128)(2,1)S(1)}, bf16[6,32,512]{2,1,0:T(8,128)(2,1)S(1)}, u32[]{:S(2)}, u32[]{:S(2)}) collective-permute-start(bf16[6,32,512]{2,1,0:T(8,128)(2,1)S(1)} %get-tuple-element.16), channel_id=1, source_target_pairs={{0,2},{1,3},{4,6},{5,7},{8,10},{9,11},{12,14},{13,15},{16,18},{17,... | collective-permute-start | bytes 589832 | tf_op jit(solution)/shard_map/ppermute | solution.py:12
  94.0 1.3 all-gather.6.cloned.1.call-done
  95.3 1.4 fusion.43
  96.7 1.5 convolution_add_fusion.14
  98.5 1.4 convolution_convert_fusion.4
  101.4 2.7 %pad_maximum_fusion = bf16[4,1,192,512]{3,0,1,2:T(4,128)(2,1)} fusion(bf16[1,1,192,512]{3,0,1,2:T(2,128)(2,1)S(1)} %copy.109, bf16[1,1,192,512]{3,0,1,2:T(2,128)(2,1)S(1)} %copy.108, bf16[1,1,192,512]{3,0,1,2:T(2,128)(2,1)S(1)} %copy.107, bf16[1,1,192,512]{3,0,1,2:T(2,128)(2,1)S(1)} %copy.106), kind=kLoop, calls=%fused_computation.58 | loop fusion | flops 3145728 | bytes 1572864 | tf_op jit(solution)/shard_map/stack | solution.py:101
  104.1 9.4 %all-to-all-start = ((bf16[4,1,192,512]{3,0,1,2:T(4,128)(2,1)}), bf16[4,1,192,512]{3,0,1,2:T(4,128)(2,1)S(1)}, u32[]{:S(2)}, u32[]{:S(2)}) async-start(bf16[4,1,192,512]{3,0,1,2:T(4,128)(2,1)} %pad_maximum_fusion), calls=%async_computation | async-start | bytes 1572864 | tf_op jit(solution)/shard_map/all_to_all | solution.py:109
  113.6 0.6 gather_fusion
  114.4 0.6 iota_compare_fusion.1
  115.0 18.2 %all-to-all-done = bf16[4,1,192,512]{3,0,1,2:T(4,128)(2,1)S(1)} async-done(((bf16[4,1,192,512]{3,0,1,2:T(4,128)(2,1)}), bf16[4,1,192,512]{3,0,1,2:T(4,128)(2,1)S(1)}, u32[]{:S(2)}, u32[]{:S(2)}) %all-to-all-start) | async-done | bytes 786464 | tf_op jit(solution)/shard_map/all_to_all | solution.py:109
  133.2 1.1 fusion.94
  134.4 0.4 fusion.61
  135.1 0.4 fusion.59
  136.1 1.2 fusion.22
  138.0 0.3 copy_bitcast_fusion
  138.3 0.7 pad_maximum_fusion.1
  139.2 21.7 %all_to_all.8 = bf16[4,4,48,512]{3,2,0,1:T(8,128)(2,1)S(1)} all-to-all(bf16[4,4,48,512]{3,2,0,1:T(8,128)(2,1)S(1)} %copy.128), channel_id=1, replica_groups=mesh['groups'=2,'space'=4,'frame'=4] {'frame'}, dimensions={1} | all-to-all | bytes 1572864 | tf_op jit(solution)/shard_map/all_to_all | solution.py:149
  160.9 0.3 convolution_add_fusion.11
  161.2 0.3 convolution_add_fusion.10
  161.6 0.3 fusion.96
  161.9 1.4 collective-permute-start.4
  163.4 1.5 collective-permute-start.5
  164.8 0.3 fusion.42
  165.2 3.3 %collective-permute-done.4 = bf16[6,32,512]{2,1,0:T(8,128)(2,1)S(1)} collective-permute-done((bf16[6,32,512]{2,1,0:T(8,128)(2,1)S(1)}, bf16[6,32,512]{2,1,0:T(8,128)(2,1)S(1)}, u32[]{:S(2)}, u32[]{:S(2)}) %collective-permute-start.4) | collective-permute-done | bytes 196640 | tf_op jit(solution)/shard_map/ppermute | solution.py:12
  168.5 0.3 convolution_add_fusion.8
  168.8 8.5 %collective-permute-done.5 = bf16[6,32,512]{2,1,0:T(8,128)(2,1)S(1)} collective-permute-done((bf16[6,32,512]{2,1,0:T(8,128)(2,1)S(1)}, bf16[6,32,512]{2,1,0:T(8,128)(2,1)S(1)}, u32[]{:S(2)}, u32[]{:S(2)}) %collective-permute-start.5) | collective-permute-done | bytes 196640 | tf_op jit(solution)/shard_map/ppermute | solution.py:12
  177.3 0.4 fusion.18
  177.7 4.4 %collective-permute-start.7 = (bf16[32,512]{1,0:T(8,128)(2,1)S(1)}, bf16[32,512]{1,0:T(8,128)(2,1)S(1)}, u32[]{:S(2)}, u32[]{:S(2)}) collective-permute-start(bf16[32,512]{1,0:T(8,128)(2,1)S(1)} %get-tuple-element.13), channel_id=1, source_target_pairs={{0,4},{4,8},{8,12},{1,5},{5,9},{9,13},{2,6},{6,10},{10,14},{3,7},{... | collective-permute-start | bytes 98312 | tf_op jit(solution)/shard_map/ppermute | solution.py:12
  182.1 1.9 collective-permute-start.6
  184.0 1.0 fusion.23
  185.0 2.3 %collective-permute-done.6 = bf16[32,512]{1,0:T(8,128)(2,1)S(1)} collective-permute-done((bf16[32,512]{1,0:T(8,128)(2,1)S(1)}, bf16[32,512]{1,0:T(8,128)(2,1)S(1)}, u32[]{:S(2)}, u32[]{:S(2)}) %collective-permute-start.6) | collective-permute-done | bytes 32800 | tf_op jit(solution)/shard_map/ppermute | solution.py:12
  187.5 0.3 fusion.40
  187.8 0.3 fusion.36
  188.1 0.3 fusion.37
  188.5 0.3 fusion.34
  188.8 0.3 convolution_add_fusion.6
  189.1 0.3 convolution_add_fusion.5
  189.5 0.3 convolution_add_fusion.4
  189.8 0.3 fusion.14
  190.2 0.4 fusion.48
  190.6 0.9 fusion.55
  (84 shorter events, 4.3 us)
Async XLA Ops:
  7.2 27.8 %copy-start.4 = (bf16[1,6,32,512]{3,2,1,0:T(8,128)(2,1)S(1)}, bf16[1,6,32,512]{3,2,1,0:T(8,128)(2,1)}, u32[]{:S(2)}) copy-start(bf16[1,6,32,512]{3,2,1,0:T(8,128)(2,1)} %param.9) | copy-start | bytes 589828
  7.2 27.8 %all-gather.8.cloned.1.call-start = ((), (), s32[]{:S(2)}) async-start(), calls=%async_computation.4 | async-start | bytes 2621440 | tf_op jit(solution)/shard_map/all_gather | solution.py:79
  7.9 66.1 %all-gather.4.cloned.1.call-start = ((), (), s32[]{:S(2)}) async-start(), calls=%async_computation.2 | async-start | bytes 5898240 | tf_op jit(solution)/shard_map/all_gather | solution.py:77
  8.7 86.6 %all-gather.6.cloned.1.call-start = ((), (), s32[]{:S(2)}) async-start(), calls=%async_computation.3 | async-start | bytes 1966080 | tf_op jit(solution)/shard_map/all_gather | solution.py:78
  14.1 7.2 %collective-permute-start.1 = (bf16[32,512]{1,0:T(8,128)(2,1)S(1)}, bf16[32,512]{1,0:T(8,128)(2,1)S(1)}, u32[]{:S(2)}, u32[]{:S(2)}) collective-permute-start(bf16[32,512]{1,0:T(8,128)(2,1)S(1)} %get-tuple-element.15), channel_id=1, source_target_pairs={{0,4},{4,8},{8,12},{1,5},{5,9},{9,13},{2,6},{6,10},{10,14},{3,7},{... | collective-permute-start | bytes 98312 | tf_op jit(solution)/shard_map/ppermute | solution.py:12
  18.6 6.5 %collective-permute-start = (bf16[32,512]{1,0:T(8,128)(2,1)S(1)}, bf16[32,512]{1,0:T(8,128)(2,1)S(1)}, u32[]{:S(2)}, u32[]{:S(2)}) collective-permute-start(bf16[32,512]{1,0:T(8,128)(2,1)S(1)} %get-tuple-element.14), channel_id=1, source_target_pairs={{4,0},{8,4},{12,8},{5,1},{9,5},{13,9},{6,2},{10,6},{14,10},{7,3},{... | collective-permute-start | bytes 98312 | tf_op jit(solution)/shard_map/ppermute | solution.py:12
  21.3 55.4 %copy-start.12 = (bf16[8]{0:T(256)(128)(2,1)}, bf16[8]{0:T(256)(128)(2,1)S(1)}, u32[]{:S(2)}) copy-start(bf16[8]{0:T(256)(128)(2,1)S(1)} %pad.22.clone) | copy-start | bytes 52
  84.6 13.6 %copy-start = (bf16[1,6,32,512]{3,2,1,0:T(8,128)(2,1)S(1)}, bf16[1,6,32,512]{3,2,1,0:T(8,128)(2,1)}, u32[]{:S(2)}) copy-start(bf16[1,6,32,512]{3,2,1,0:T(8,128)(2,1)} %param.8) | copy-start | bytes 589828
  86.8 9.9 %collective-permute-start.2 = (bf16[6,32,512]{2,1,0:T(8,128)(2,1)S(1)}, bf16[6,32,512]{2,1,0:T(8,128)(2,1)S(1)}, u32[]{:S(2)}, u32[]{:S(2)}) collective-permute-start(bf16[6,32,512]{2,1,0:T(8,128)(2,1)S(1)} %get-tuple-element.16), channel_id=1, source_target_pairs={{0,1},{1,2},{2,3},{4,5},{5,6},{6,7},{8,9},{9,10},{10,11},{12,13},{... | collective-permute-start | bytes 589832 | tf_op jit(solution)/shard_map/ppermute | solution.py:12
  89.9 8.2 %collective-permute-start.3 = (bf16[6,32,512]{2,1,0:T(8,128)(2,1)S(1)}, bf16[6,32,512]{2,1,0:T(8,128)(2,1)S(1)}, u32[]{:S(2)}, u32[]{:S(2)}) collective-permute-start(bf16[6,32,512]{2,1,0:T(8,128)(2,1)S(1)} %get-tuple-element.16), channel_id=1, source_target_pairs={{0,2},{1,3},{4,6},{5,7},{8,10},{9,11},{12,14},{13,15},{16,18},{17,... | collective-permute-start | bytes 589832 | tf_op jit(solution)/shard_map/ppermute | solution.py:12
  95.2 2.9 %copy-start.1 = (bf16[3,512,512]{2,1,0:T(8,128)(2,1)S(1)}, bf16[3,512,512]{2,1,0:T(8,128)(2,1)}, u32[]{:S(2)}) copy-start(bf16[3,512,512]{2,1,0:T(8,128)(2,1)} %all-gather.6.cloned.1.call-done) | copy-start | bytes 4718596
  96.7 3.5 %copy-start.2 = (bf16[4,512,512]{2,1,0:T(8,128)(2,1)S(1)}, bf16[4,512,512]{2,1,0:T(8,128)(2,1)}, u32[]{:S(2)}) copy-start(bf16[4,512,512]{2,1,0:T(8,128)(2,1)} %all-gather.8.cloned.1.call-done) | copy-start | bytes 6291460
  98.5 2.6 %copy-start.8 = (bf16[6,32,512]{2,1,0:T(8,128)(2,1)}, bf16[6,32,512]{2,1,0:T(8,128)(2,1)S(1)}, u32[]{:S(2)}) copy-start(bf16[6,32,512]{2,1,0:T(8,128)(2,1)S(1)} %fusion.17) | copy-start | bytes 589828
  101.4 12.2 %copy-start.11 = (s32[4,32]{1,0:T(4,128)S(1)}, s32[4,32]{1,0:T(4,128)}, u32[]{:S(2)}) copy-start(s32[4,32]{1,0:T(4,128)} %param.11) | copy-start | bytes 1540
  104.1 29.1 %all-to-all-start = ((bf16[4,1,192,512]{3,0,1,2:T(4,128)(2,1)}), bf16[4,1,192,512]{3,0,1,2:T(4,128)(2,1)S(1)}, u32[]{:S(2)}, u32[]{:S(2)}) async-start(bf16[4,1,192,512]{3,0,1,2:T(4,128)(2,1)} %pad_maximum_fusion), calls=%async_computation | async-start | bytes 1572864 | tf_op jit(solution)/shard_map/all_to_all | solution.py:109
  134.4 0.7 copy-start.5
  134.4 1.2 copy-start.14
  135.1 0.8 copy-start.7
  135.1 2.2 %copy-start.6 = (bf16[1,1,192,512]{3,2,1,0:T(8,128)(2,1)S(1)}, bf16[1,1,192,512]{3,2,1,0:T(8,128)(2,1)}, u32[]{:S(2)}) copy-start(bf16[1,1,192,512]{3,2,1,0:T(8,128)(2,1)} %copy-done.5) | copy-start | bytes 589828
  139.0 21.9 %copy-start.3 = (bf16[4,512,512]{2,1,0:T(8,128)(2,1)S(1)}, bf16[4,512,512]{2,1,0:T(8,128)(2,1)}, u32[]{:S(2)}) copy-start(bf16[4,512,512]{2,1,0:T(8,128)(2,1)} %all-gather.8.cloned.1.call-done) | copy-start | bytes 6291460
  160.8 26.6 %slice-start = ((s8[4718592]{0:T(1024)(128)(4,1)}), s8[4194304]{0:T(1024)(128)(4,1)S(1)}, s32[]{:S(2)}) async-start(s8[4718592]{0:T(1024)(128)(4,1)} %bitcast.196), calls=%async_computation.5 | async-start | bytes 8388608
  161.6 15.7 %copy-start.15 = (f32[6,32,512]{2,1,0:T(8,128)S(1)}, f32[6,32,512]{2,1,0:T(8,128)}, u32[]{:S(2)}) copy-start(f32[6,32,512]{2,1,0:T(8,128)} %get-tuple-element.17) | copy-start | bytes 1179652
  161.9 25.5 %slice-start.1 = ((s8[4718592]{0:T(1024)(128)(4,1)}), s8[524288]{0:T(1024)(128)(4,1)S(1)}, s32[]{:S(2)}) async-start(s8[4718592]{0:T(1024)(128)(4,1)} %bitcast.196), calls=%async_computation.6 | async-start | bytes 1048576
  161.9 6.5 %collective-permute-start.4 = (bf16[6,32,512]{2,1,0:T(8,128)(2,1)S(1)}, bf16[6,32,512]{2,1,0:T(8,128)(2,1)S(1)}, u32[]{:S(2)}, u32[]{:S(2)}) collective-permute-start(bf16[6,32,512]{2,1,0:T(8,128)(2,1)S(1)} %get-tuple-element.20), channel_id=1, source_target_pairs={{1,0},{2,1},{3,2},{5,4},{6,5},{7,6},{9,8},{10,9},{11,10},{13,12},{... | collective-permute-start | bytes 589832 | tf_op jit(solution)/shard_map/ppermute | solution.py:12
  163.4 13.9 %collective-permute-start.5 = (bf16[6,32,512]{2,1,0:T(8,128)(2,1)S(1)}, bf16[6,32,512]{2,1,0:T(8,128)(2,1)S(1)}, u32[]{:S(2)}, u32[]{:S(2)}) collective-permute-start(bf16[6,32,512]{2,1,0:T(8,128)(2,1)S(1)} %get-tuple-element.20), channel_id=1, source_target_pairs={{2,0},{3,1},{6,4},{7,5},{10,8},{11,9},{14,12},{15,13},{18,16},{19,... | collective-permute-start | bytes 589832 | tf_op jit(solution)/shard_map/ppermute | solution.py:12
  165.2 18.9 %copy-start.9 = (bf16[6,32,512]{2,1,0:T(8,128)(2,1)S(1)}, bf16[6,32,512]{2,1,0:T(8,128)(2,1)}, u32[]{:S(2)}) copy-start(bf16[6,32,512]{2,1,0:T(8,128)(2,1)} %copy-done.8) | copy-start | bytes 589828
  177.3 10.0 %copy-start.13 = (bf16[8]{0:T(256)(128)(2,1)S(1)}, bf16[8]{0:T(256)(128)(2,1)}, u32[]{:S(2)}) copy-start(bf16[8]{0:T(256)(128)(2,1)} %copy-done.12) | copy-start | bytes 52
  177.7 7.3 %collective-permute-start.7 = (bf16[32,512]{1,0:T(8,128)(2,1)S(1)}, bf16[32,512]{1,0:T(8,128)(2,1)S(1)}, u32[]{:S(2)}, u32[]{:S(2)}) collective-permute-start(bf16[32,512]{1,0:T(8,128)(2,1)S(1)} %get-tuple-element.13), channel_id=1, source_target_pairs={{0,4},{4,8},{8,12},{1,5},{5,9},{9,13},{2,6},{6,10},{10,14},{3,7},{... | collective-permute-start | bytes 98312 | tf_op jit(solution)/shard_map/ppermute | solution.py:12
  182.1 5.2 %collective-permute-start.6 = (bf16[32,512]{1,0:T(8,128)(2,1)S(1)}, bf16[32,512]{1,0:T(8,128)(2,1)S(1)}, u32[]{:S(2)}, u32[]{:S(2)}) collective-permute-start(bf16[32,512]{1,0:T(8,128)(2,1)S(1)} %get-tuple-element.12), channel_id=1, source_target_pairs={{4,0},{8,4},{12,8},{5,1},{9,5},{13,9},{6,2},{10,6},{14,10},{7,3},{... | collective-permute-start | bytes 98312 | tf_op jit(solution)/shard_map/ppermute | solution.py:12
  189.5 0.7 copy-start.10
Sparse Core Ops, SparseCore 0:
  9.5 25.3 all-gather.7
  36.5 37.4 all-gather.3
  75.6 19.6 all-gather.5
where the time goes:
time: 199 us; the launch traced here: 198 us
  waiting for transfers between devices  85.9 us (43%)
  starting transfers between devices  32.3 us (16%)
  matrix products  27.3 us (14%)
  blocking collectives  21.7 us (11%)
  between operations  16.4 us (8%)
  other arithmetic  8.6 us (4%)
  local copies, waits for them, and re-layouts  5.75 us (3%)
    all_gather x1, waiting for transfers between devices, per_device(): lax.all_gather(w_spatial, 'space', axis=1, tiled=True)  37.3 us
    ppermute x8, starting transfers between devices, passed_along(): lax.ppermute(value, axis, [(source, source + steps) for source in range(f...  22.8 us
    all_to_all x1, blocking collectives, per_device(): lax.all_to_all(returning, 'frame', split_axis=1, concat_axis=2, tiled=True)  21.7 us
    all_to_all x1, waiting for transfers between devices, per_device(): lax.all_to_all(outgoing, 'frame', split_axis=2, concat_axis=1, tiled=True)  18.2 us
    ppermute x8, waiting for transfers between devices, passed_along(): lax.ppermute(value, axis, [(source, source + steps) for source in range(f...  17.9 us
    dot_general x9, matrix products, spatial_conv(): jnp.einsum('hwd,de->hwe', patches, kernel[tap_row * 3 + tap_col], preferr...  12.8 us
    all_gather x1, waiting for transfers between devices, per_device(): lax.all_gather(w_attn, 'space', axis=1, tiled=True)  9.82 us
    all_to_all x1, starting transfers between devices, per_device(): lax.all_to_all(outgoing, 'frame', split_axis=2, concat_axis=1, tiled=True)  9.44 us
  transfers between devices with their start and end apart: 12, of which 8 were waited for; matrix products, arithmetic and copies ran while one was open for 12% of the time, Pallas kernels for 0%

commit v1 on v0

--- a/solution.py
+++ b/solution.py
@@ -1,6 +1,10 @@
+import functools
+
 import jax
 import jax.numpy as jnp
 from jax import lax
+from jax.experimental import pallas as pl
+from jax.experimental.pallas import tpu as pltpu
 from jax.sharding import PartitionSpec as P
 
 NORM_EPSILON = 1e-06
@@ -180,6 +184,502 @@
     return (block_output[None], clip_grad[None])
 
 
+MESH_ID = pl.DeviceIdType.MESH
+LOW = jnp.bfloat16
+WIDE = jnp.float32
+ROW_PAD = 16
+SLOT_PAD = 8
+
+
+def dot_plain(left, right):
+    return jnp.dot(left, right, preferred_element_type=WIDE)
+
+
+def dot_back(left, right):
+    return lax.dot_general(left, right, (((1,), (1,)), ((), ())), preferred_element_type=WIDE)
+
+
+def strip_kernel(
+    n, frames, cs, cf, taps_total,
+    pick, place, gain, bias, keep, clip_in, cot_in, ws_in, wt_in, wa_in,
+    out_block, out_grad,
+    weights, clip_slab, cot_slab, clip_comp, cot_comp, clip_all, cot_all,
+    shifted, pre, act_pad, resid, qs, ks, gs, att, gres, glow_pad, ghid,
+    block_own, grad_own, block_z, grad_z, block_slab, grad_slab,
+    x_s, x_r, c0_s, c0_r, y_s, y_r, c1_s, c1_r, c2_s, c2_r, w_loc,
+    p1_s, p1_r, p1_l, p2_s, p2_r, p2_l, oz_s, oz_r, oz_l, ox_s, ox_r, ox_l,
+):
+    space = lax.axis_index("space")
+    frame = lax.axis_index("frame")
+    group = lax.axis_index("groups")
+    chip = space // 2
+    core = space % 2
+    partner = chip * 2 + 1 - core
+    across = (1 - chip) * 2 + core
+    across_other = (1 - chip) * 2 + 1 - core
+    wide = cf + 2
+    full = ROW_PAD * frames
+    depth = ws_in.shape[1]
+    channels = ws_in.shape[2]
+    half = depth // 2
+    scale = channels ** (-0.5)
+
+    def remote(src, dst, ssem, rsem, where):
+        return pltpu.make_async_remote_copy(
+            src_ref=src, dst_ref=dst, send_sem=ssem, recv_sem=rsem,
+            device_id=where, device_id_type=MESH_ID,
+        )
+
+    barrier = pltpu.get_barrier_semaphore()
+    for k in range(1, n):
+        pl.semaphore_signal(barrier, inc=1, device_id={"space": (space + k) % n}, device_id_type=MESH_ID)
+    for k in range(1, frames):
+        pl.semaphore_signal(barrier, inc=1, device_id={"frame": (frame + k) % frames}, device_id_type=MESH_ID)
+    pl.semaphore_signal(barrier, inc=1, device_id={"groups": 1 - group}, device_id_type=MESH_ID)
+    pl.semaphore_wait(barrier, n + frames - 1)
+
+    def p1_copy(which, k):
+        source, slab, grow = ((clip_in, clip_slab, 4), (cot_in, cot_slab, 2))[which]
+        to = (space + k) % n
+        return remote(
+            source.at[pl.ds(cs * to, cs + grow)], slab.at[:, space],
+            p1_s.at[which, k - 1], p1_r.at[which, k - 1], {"space": to},
+        )
+
+    def p1_arrival(which, k):
+        slab = (clip_slab, cot_slab)[which]
+        came = (space - k + n) % n
+        return remote(slab.at[:, came], slab.at[:, came], p1_s.at[which, k - 1], p1_r.at[which, k - 1], {"space": came})
+
+    def p1_local(which):
+        source, slab, grow = ((clip_in, clip_slab, 4), (cot_in, cot_slab, 2))[which]
+        return pltpu.make_async_copy(source.at[pl.ds(cs * space, cs + grow)], slab.at[:, space], p1_l.at[which])
+
+    sources = (
+        [(ws_in, i) for i in range(ws_in.shape[0])]
+        + [(wt_in, i) for i in range(wt_in.shape[0])]
+        + [(wa_in, i) for i in range(wa_in.shape[0])]
+    )
+    first_temporal = ws_in.shape[0]
+    first_attn = first_temporal + wt_in.shape[0]
+    total = len(sources)
+    my_rows = pl.ds(pl.multiple_of(group * half, half), half)
+    other_rows = pl.ds(pl.multiple_of((1 - group) * half, half), half)
+
+    def x_copy(m):
+        ref, i = sources[m]
+        return remote(ref.at[i, my_rows], weights.at[m, space, my_rows], x_s.at[m], x_r.at[m], {"space": across})
+
+    def c0_copy(m):
+        ref, i = sources[m]
+        return remote(ref.at[i], weights.at[m, space], c0_s.at[m], c0_r.at[m], {"space": partner})
+
+    def local_copy(m):
+        ref, i = sources[m]
+        return pltpu.make_async_copy(ref.at[i], weights.at[m, space], w_loc.at[m])
+
+    for which in range(2):
+        for k in range(1, n):
+            p1_copy(which, k).start()
+        p1_local(which).start()
+    for m in range(total):
+        x_copy(m).start()
+        c0_copy(m).start()
+        local_copy(m).start()
+
+    def y_copy(m):
+        piece = weights.at[m, across, my_rows]
+        return remote(piece, piece, y_s.at[m], y_r.at[m], {"groups": 1 - group})
+
+    def c1_copy(m):
+        piece = weights.at[m, across, my_rows]
+        return remote(piece, piece, c1_s.at[m], c1_r.at[m], {"space": partner})
+
+    def c2_copy(m):
+        piece = weights.at[m, across, other_rows]
+        return remote(piece, piece, c2_s.at[m], c2_r.at[m], {"space": partner})
+
+    def arrival(m, owner, rows, ssem, rsem, where):
+        piece = weights.at[m, owner, rows] if rows is not None else weights.at[m, owner]
+        return remote(piece, piece, ssem.at[m], rsem.at[m], where)
+
+    def relay_first(m):
+        arrival(m, across, my_rows, x_s, x_r, {"space": across}).wait_recv()
+        y_copy(m).start()
+        c1_copy(m).start()
+
+    def relay_second(m):
+        arrival(m, across, other_rows, y_s, y_r, {"groups": 1 - group}).wait_recv()
+        c2_copy(m).start()
+
+    def ready(m):
+        arrival(m, partner, None, c0_s, c0_r, {"space": partner}).wait_recv()
+        arrival(m, across_other, my_rows, c1_s, c1_r, {"space": partner}).wait_recv()
+        arrival(m, across_other, other_rows, c2_s, c2_r, {"space": partner}).wait_recv()
+
+    def compact(which):
+        slab, comp = ((clip_slab, clip_comp), (cot_slab, cot_comp))[which]
+        for k in range(1, n):
+            p1_arrival(which, k).wait_recv()
+        p1_local(which).wait()
+
+        @pl.loop(0, slab.shape[0])
+        def _(col):
+            rows = jnp.concatenate([slab[col, t].astype(WIDE) for t in range(n)], 0).astype(LOW)
+            comp[col] = dot_plain(pick[...], rows).astype(LOW)
+
+    def p2_copy(which, k):
+        comp, whole, grow = ((clip_comp, clip_all, 4), (cot_comp, cot_all, 2))[which]
+        to = (frame + k) % frames
+        return remote(
+            comp.at[pl.ds(cf * to, cf + grow)], whole.at[:, frame],
+            p2_s.at[which, k - 1], p2_r.at[which, k - 1], {"frame": to},
+        )
+
+    def p2_arrival(which, k):
+        whole = (clip_all, cot_all)[which]
+        came = (frame - k + frames) % frames
+        return remote(whole.at[:, came], whole.at[:, came], p2_s.at[which, k - 1], p2_r.at[which, k - 1], {"frame": came})
+
+    def p2_local(which):
+        comp, whole, grow = ((clip_comp, clip_all, 4), (cot_comp, cot_all, 2))[which]
+        return pltpu.make_async_copy(comp.at[pl.ds(cf * frame, cf + grow)], whole.at[:, frame], p2_l.at[which])
+
+    for which in range(2):
+        compact(which)
+        for k in range(1, frames):
+            p2_copy(which, k).start()
+        p2_local(which).start()
+
+    act_pad[:, 0:2] = jnp.zeros((wide, 2, ROW_PAD, channels), LOW)
+    glow_pad[:, frames : frames + 2] = jnp.zeros((wide, 2, ROW_PAD, channels), LOW)
+    for k in range(1, frames):
+        p2_arrival(0, k).wait_recv()
+    p2_local(0).wait()
+
+    @pl.loop(0, wide + 2)
+    def _(col):
+        x = clip_all[col].reshape(full, channels).astype(WIDE)
+        inverse = lax.rsqrt(jnp.mean(x * x, -1, keepdims=True) + NORM_EPSILON)
+        h = x * inverse * gain[...]
+        shifted[0, col] = pltpu.roll(h, 1, 0).astype(LOW)
+        shifted[1, col] = h.astype(LOW)
+        shifted[2, col] = pltpu.roll(h, full - 1, 0).astype(LOW)
+
+    pre[...] = jnp.zeros_like(pre)
+    for m in range(total):
+        local_copy(m).wait()
+
+    def weight(m):
+        return weights[m].reshape(n * depth, channels)
+
+    relay_first(0)
+
+    @pl.loop(0, taps_total)
+    def _(m):
+        relay_first(m + 1)
+        relay_second(m)
+        ready(m)
+        lhs = shifted[m // 3, pl.ds(m % 3, wide)].reshape(wide * full, channels)
+        pre[...] += dot_plain(lhs, weight(m))
+
+    for m in range(taps_total + 1, total):
+        relay_first(m)
+    for m in range(taps_total, total):
+        relay_second(m)
+
+    @pl.loop(0, wide)
+    def _(col):
+        p = pre[pl.ds(col * full, full)]
+        act_pad[col, pl.ds(2, frames)] = (p * jax.nn.sigmoid(p)).astype(LOW).reshape(frames, ROW_PAD, channels)
+
+    for k in range(1, frames):
+        p2_arrival(1, k).wait_recv()
+    p2_local(1).wait()
+    for m in range(taps_total, total):
+        ready(m)
+
+    def flat(ref, lo, count):
+        return ref[pl.ds(lo, count)].reshape(count * full, channels)
+
+    mixed = flat(clip_all, 1, wide).astype(WIDE)
+    for k in range(wt_in.shape[0]):
+        mixed += dot_plain(
+            act_pad[:, pl.ds(2 - k, frames)].reshape(wide * full, channels), weight(first_temporal + k)
+        )
+    low = mixed.astype(LOW)
+    resid[...] = low.reshape(resid.shape)
+
+    @pl.loop(0, 3)
+    def _(i):
+        qs[i] = dot_plain(flat(resid, 0, wide), weight(first_attn + i)).astype(LOW).reshape(resid.shape)
+
+    gs[...] = dot_back(flat(cot_all, 0, wide), weight(first_attn + 3)).astype(LOW).reshape(resid.shape)
+
+    @pl.loop(0, wide)
+    def _(col):
+        q = [qs[0, col, f].astype(WIDE) for f in range(frames)]
+        kk = [qs[1, col, f].astype(WIDE) for f in range(frames)]
+        v = [qs[2, col, f].astype(WIDE) for f in range(frames)]
+        up = [gs[col, f].astype(WIDE) for f in range(frames)]
+        gk = [None] * frames
+        gv = [None] * frames
+        for f in range(frames):
+            sc = [
+                jnp.sum(q[f] * kk[g], -1, keepdims=True) * scale + bias[col, f * frames + g][:, :1]
+                for g in range(f + 1)
+            ]
+            top = sc[0]
+            for g in range(1, f + 1):
+                top = jnp.maximum(top, sc[g])
+            ex = [jnp.exp(s - top) for s in sc]
+            den = ex[0]
+            for g in range(1, f + 1):
+                den = den + ex[g]
+            pr = [e / den for e in ex]
+            gp = [jnp.sum(up[f] * v[g], -1, keepdims=True) for g in range(f + 1)]
+            dot_sum = pr[0] * gp[0]
+            for g in range(1, f + 1):
+                dot_sum = dot_sum + pr[g] * gp[g]
+            a = None
+            gq = None
+            for g in range(f + 1):
+                pl_low = pr[g].astype(LOW).astype(WIDE)
+                sg = (pr[g] * (gp[g] - dot_sum)).astype(LOW).astype(WIDE)
+                a = pl_low * v[g] if a is None else a + pl_low * v[g]
+                gq = sg * kk[g] if gq is None else gq + sg * kk[g]
+                tk = (sg * q[f] * scale).astype(LOW).astype(WIDE)
+                tv = (pl_low * up[f]).astype(LOW).astype(WIDE)
+                gk[g] = tk if gk[g] is None else gk[g] + tk
+                gv[g] = tv if gv[g] is None else gv[g] + tv
+            att[col, f] = a.astype(LOW)
+            ks[0, col, f] = (gq * scale).astype(LOW)
+        for g in range(frames):
+            ks[1, col, g] = gk[g].astype(LOW)
+            ks[2, col, g] = gv[g].astype(LOW)
+
+    def spread(own, values):
+        for c in range(cf):
+            own[:, c] = values[c * full : (c + 1) * full].astype(LOW).reshape(frames, ROW_PAD, channels)
+
+    block = flat(resid, 1, cf).astype(WIDE) + dot_plain(flat(att, 1, cf), weight(first_attn + 3))
+    spread(block_own, block)
+
+    def oz_copy(which, k):
+        own, z = ((block_own, block_z), (grad_own, grad_z))[which]
+        to = (frame + k) % frames
+        return remote(own.at[to], z.at[frame], oz_s.at[which, k - 1], oz_r.at[which, k - 1], {"frame": to})
+
+    def oz_arrival(which, k):
+        z = (block_z, grad_z)[which]
+        came = (frame - k + frames) % frames
+        return remote(z.at[came], z.at[came], oz_s.at[which, k - 1], oz_r.at[which, k - 1], {"frame": came})
+
+    def oz_local(which):
+        own, z = ((block_own, block_z), (grad_own, grad_z))[which]
+        return pltpu.make_async_copy(own.at[frame], z.at[frame], oz_l.at[which])
+
+    def ox_copy(which, k):
+        slab, out = ((block_slab, out_block), (grad_slab, out_grad))[which]
+        to = (space + k) % n
+        return remote(
+            slab.at[to], out.at[pl.ds(cs * space, cs)], ox_s.at[which, k - 1], ox_r.at[which, k - 1], {"space": to}
+        )
+
+    def ox_arrival(which, k):
+        out = (out_block, out_grad)[which]
+        came = (space - k + n) % n
+        piece = out.at[pl.ds(cs * came, cs)]
+        return remote(piece, piece, ox_s.at[which, k - 1], ox_r.at[which, k - 1], {"space": came})
+
+    def ox_local(which):
+        slab, out = ((block_slab, out_block), (grad_slab, out_grad))[which]
+        return pltpu.make_async_copy(slab.at[space], out.at[pl.ds(cs * space, cs)], ox_l.at[which])
+
+    def send_frames(which):
+        for k in range(1, frames):
+            oz_copy(which, k).start()
+        oz_local(which).start()
+
+    def send_tiles(which):
+        z, slab = ((block_z, block_slab), (grad_z, grad_slab))[which]
+        for k in range(1, frames):
+            oz_arrival(which, k).wait_recv()
+        oz_local(which).wait()
+
+        @pl.loop(0, frames)
+        def _(f):
+            for c in range(cf):
+                rows = dot_plain(place[...], z[f, c])
+                for t in range(n):
+                    slab[t, f * cf + c] = rows[t * SLOT_PAD : (t + 1) * SLOT_PAD].astype(LOW)
+
+        for k in range(1, n):
+            ox_copy(which, k).start()
+        ox_local(which).start()
+
+    send_frames(0)
+    gres[...] = flat(cot_all, 0, wide).astype(WIDE)
+
+    @pl.loop(0, 3)
+    def _(i):
+        gres[...] += dot_back(flat(ks.at[i], 0, wide), weight(first_attn + i))
+
+    glow_pad[:, pl.ds(0, frames)] = gres[...].astype(LOW).reshape(resid.shape)
+    send_tiles(0)
+    gact = None
+    for k in range(wt_in.shape[0]):
+        term = dot_back(glow_pad[:, pl.ds(k, frames)].reshape(wide * full, channels), weight(first_temporal + k))
+        gact = term if gact is None else gact + term
+    pre_all = pre[...]
+    sig = jax.nn.sigmoid(pre_all)
+    pre[...] = gact * sig * (1.0 + pre_all * (1.0 - sig))
+
+    @pl.loop(0, wide)
+    def _(col):
+        p = jnp.where(keep[col][:, :1] > 0.5, pre[pl.ds(col * full, full)], 0.0)
+        shifted[0, col] = pltpu.roll(p, 1, 0).astype(LOW)
+        shifted[1, col] = p.astype(LOW)
+        shifted[2, col] = pltpu.roll(p, full - 1, 0).astype(LOW)
+
+    ghid[...] = jnp.zeros_like(ghid)
+
+    @pl.loop(0, taps_total)
+    def _(m):
+        lhs = shifted[2 - m // 3, pl.ds(2 - m % 3, cf)].reshape(cf * full, channels)
+        ghid[...] += dot_back(lhs, weight(m))
+
+    for c in range(cf):
+        x = clip_all[c + 2].reshape(full, channels).astype(WIDE)
+        inverse = lax.rsqrt(jnp.mean(x * x, -1, keepdims=True) + NORM_EPSILON)
+        normed = x * inverse
+        gn = ghid[c * full : (c + 1) * full] * gain[...]
+        back = inverse * (gn - normed * jnp.mean(gn * normed, -1, keepdims=True))
+        result = gres[(c + 1) * full : (c + 2) * full] + back
+        grad_own[:, c] = result.astype(LOW).reshape(frames, ROW_PAD, channels)
+
+    send_frames(1)
+    send_tiles(1)
+    for which in range(2):
+        for k in range(1, n):
+            ox_arrival(which, k).wait_recv()
+        ox_local(which).wait()
+        for k in range(1, n):
+            p1_copy(which, k).wait_send()
+            ox_copy(which, k).wait_send()
+        for k in range(1, frames):
+            p2_copy(which, k).wait_send()
+            oz_copy(which, k).wait_send()
+    for m in range(total):
+        x_copy(m).wait_send()
+        c0_copy(m).wait_send()
+        y_copy(m).wait_send()
+        c1_copy(m).wait_send()
+        c2_copy(m).wait_send()
+
+
+def per_device_strips(clip, cotangent, tile_rows, frame_start, norm_gain, w_spatial, w_temporal, w_attn):
+    slots = clip.shape[1]
+    breadth = clip.shape[2]
+    channels = clip.shape[3]
+    n = lax.axis_size("space")
+    frames = lax.axis_size("frame")
+    space = lax.axis_index("space")
+    frame = lax.axis_index("frame")
+    cs = breadth // n
+    cf = cs // frames
+    wide = cf + 2
+    full = ROW_PAD * frames
+    depth = w_spatial.shape[1]
+    taps_total = w_spatial.shape[0]
+    total = taps_total + w_temporal.shape[0] + w_attn.shape[0]
+    bounds = jnp.cumsum(tile_rows) - tile_rows
+    slot_ids = jnp.arange(SLOT_PAD)
+    row_of = jnp.where(slot_ids[None, :] < tile_rows[:, None], bounds[:, None] + slot_ids[None, :], -1).reshape(-1)
+    place = (row_of[:, None] == jnp.arange(ROW_PAD)[None, :]).astype(LOW)
+    pick = (row_of[None, :] == jnp.arange(ROW_PAD)[:, None]).astype(LOW)
+    columns = space * cs + frame * cf - 1 + jnp.arange(wide)
+    inside = (columns >= 0) & (columns < breadth)
+    starts = jnp.take(frame_start, jnp.clip(columns, 0, breadth - 1), axis=1)
+    bias = jnp.where(starts.T[:, :, None] <= jnp.arange(frames)[None, None, :], 0.0, -1e30).astype(WIDE)
+    bias = jnp.broadcast_to(bias.reshape(wide, frames * frames, 1, 1), (wide, frames * frames, 1, 128))
+    live_row = (jnp.arange(full) % ROW_PAD) < jnp.sum(tile_rows)
+    keep = jnp.broadcast_to(
+        (inside[:, None] & live_row[None, :]).astype(WIDE)[:, :, None], (wide, full, 128)
+    )
+    def by_column(values, halo):
+        turned = jnp.transpose(values[0], (1, 0, 2))
+        return jnp.pad(turned, ((halo, halo), (0, SLOT_PAD - slots), (0, 0)))
+
+    vmem = pl.BlockSpec(memory_space=pltpu.VMEM)
+    hbm = pl.BlockSpec(memory_space=pl.ANY)
+    dma = pltpu.SemaphoreType.DMA
+    shape4 = (frames, ROW_PAD, channels)
+    scratch = [
+        pltpu.VMEM((total, n, depth, channels), LOW),
+        pltpu.VMEM((cs + 4, n, SLOT_PAD, channels), LOW),
+        pltpu.VMEM((cs + 2, n, SLOT_PAD, channels), LOW),
+        pltpu.VMEM((cs + 4, ROW_PAD, channels), LOW),
+        pltpu.VMEM((cs + 2, ROW_PAD, channels), LOW),
+        pltpu.VMEM((wide + 2,) + shape4, LOW),
+        pltpu.VMEM((wide,) + shape4, LOW),
+        pltpu.VMEM((3, wide + 2, full, channels), LOW),
+        pltpu.VMEM((wide * full, channels), WIDE),
+        pltpu.VMEM((wide, frames + 2, ROW_PAD, channels), LOW),
+        pltpu.VMEM((wide,) + shape4, LOW),
+        pltpu.VMEM((3, wide) + shape4, LOW),
+        pltpu.VMEM((3, wide) + shape4, LOW),
+        pltpu.VMEM((wide,) + shape4, LOW),
+        pltpu.VMEM((wide,) + shape4, LOW),
+        pltpu.VMEM((wide * full, channels), WIDE),
+        pltpu.VMEM((wide, frames + 2, ROW_PAD, channels), LOW),
+        pltpu.VMEM((cf * full, channels), WIDE),
+        pltpu.VMEM((frames, cf, ROW_PAD, channels), LOW),
+        pltpu.VMEM((frames, cf, ROW_PAD, channels), LOW),
+        pltpu.VMEM((frames, cf, ROW_PAD, channels), LOW),
+        pltpu.VMEM((frames, cf, ROW_PAD, channels), LOW),
+        pltpu.VMEM((n, cs, SLOT_PAD, channels), LOW),
+        pltpu.VMEM((n, cs, SLOT_PAD, channels), LOW),
+    ]
+    scratch += [dma((total,)) for _ in range(11)]
+    scratch += [dma((2, n - 1)), dma((2, n - 1)), dma((2,))]
+    scratch += [dma((2, frames - 1)), dma((2, frames - 1)), dma((2,))] * 2
+    scratch += [dma((2, n - 1)), dma((2, n - 1)), dma((2,))]
+    out = jax.ShapeDtypeStruct((breadth, SLOT_PAD, channels), LOW)
+    block, grad = pl.pallas_call(
+        functools.partial(strip_kernel, n, frames, cs, cf, taps_total),
+        out_shape=(out, out),
+        in_specs=[vmem] * 5 + [hbm] * 5,
+        out_specs=(vmem, vmem),
+        scratch_shapes=scratch,
+        compiler_params=pltpu.CompilerParams(
+            collective_id=0, has_side_effects=True, vmem_limit_bytes=48 * 1024 * 1024
+        ),
+    )(
+        pick, place, norm_gain.reshape(1, channels), bias, keep,
+        by_column(clip, 2), by_column(cotangent, 1), w_spatial, w_temporal, w_attn,
+    )
+
+    def by_slot(values):
+        return jnp.transpose(values[:, :slots], (1, 0, 2))[None]
+
+    return by_slot(block), by_slot(grad)
+
+
+def strips_fit(mesh, clip, tile_rows):
+    n = mesh.shape["space"]
+    frames = mesh.shape["frame"]
+    slots_all, breadth, channels = clip.shape[1:]
+    return (
+        mesh.shape["groups"] == 2
+        and n == 4
+        and breadth % (n * frames) == 0
+        and slots_all // n <= SLOT_PAD
+        and slots_all // 2 < ROW_PAD
+        and channels % (128 * n) == 0
+    )
+
+
 def solution(mesh):
     placed = (
         P(("groups", "frame"), "space", None, None),
@@ -191,13 +691,18 @@
         P(None, "space", None),
         P(None, "space", None),
     )
-    return jax.shard_map(
-        per_device,
-        mesh=mesh,
-        in_specs=placed,
-        out_specs=(
-            P(("groups", "frame"), "space", None, None),
-            P(("groups", "frame"), "space", None, None),
-        ),
-        check_vma=False,
-    )
+
+    def run(*arrays):
+        fits = strips_fit(mesh, arrays[0], arrays[2])
+        return jax.shard_map(
+            per_device_strips if fits else per_device,
+            mesh=mesh,
+            in_specs=placed,
+            out_specs=(
+                P(("groups", "frame"), "space", None, None),
+                P(("groups", "frame"), "space", None, None),
+            ),
+            check_vma=False,
+        )(*arrays)
+
+    return run

time: 199 us -> 93 us (0.47)
  waiting for transfers between devices: 85.9 us -> 0 us
  Pallas kernels: 0 us -> 82.5 us
  starting transfers between devices: 32.3 us -> 0 us
  matrix products: 27.3 us -> 0 us
  blocking collectives: 21.7 us -> 0 us
  between operations: 16.4 us -> 0.78 us
  other arithmetic: 8.6 us -> 3.9 us
    pallas_call x0 -> x1, Pallas kernels: none -> 82.5 us  [per_device_strips(): pl.pallas_call(functools.partial(strip_kernel, n, frames, cs, cf, taps_to...]
    all_gather x3 -> x0, waiting for transfers between devices: 48.4 us -> none  [the longest x1 37.3 us: per_device(): lax.all_gather(w_spatial, 'space', axis=1, tiled=True)]
    dot_general x36 -> x0, matrix products: 27.3 us -> none  [the longest x9 12.8 us: spatial_conv(): jnp.einsum('hwd,de->hwe', patches, kernel[tap_row * 3 + tap_col], preferr...]
    ppermute x8 -> x0, starting transfers between devices: 22.8 us -> none  [passed_along(): lax.ppermute(value, axis, [(source, source + steps) for source in range(f...]
    all_to_all x1 -> x0, blocking collectives: 21.7 us -> none  [per_device(): lax.all_to_all(returning, 'frame', split_axis=1, concat_axis=2, tiled=True)]
    all_to_all x1 -> x0, waiting for transfers between devices: 18.2 us -> none  [per_device(): lax.all_to_all(outgoing, 'frame', split_axis=2, concat_axis=1, tiled=True)]
    ppermute x8 -> x0, waiting for transfers between devices: 17.9 us -> none  [passed_along(): lax.ppermute(value, axis, [(source, source + steps) for source in range(f...]
    all_to_all x1 -> x0, starting transfers between devices: 9.44 us -> none  [per_device(): lax.all_to_all(outgoing, 'frame', split_axis=2, concat_axis=1, tiled=True)]
  transfers between devices with their start and end apart: 12 -> 0, of which waited for: 8 -> 0; matrix products, arithmetic and copies ran while one was open for 12% -> 0% of each run, Pallas kernels for 0% -> 0%
where the time goes in v1:
time: 93 us; the launch traced here: 92.8 us
  Pallas kernels  82.5 us (89%)
  local copies, waits for them, and re-layouts  5.59 us (6%)
  other arithmetic  3.9 us (4%)
    pallas_call x1, Pallas kernels, per_device_strips(): pl.pallas_call(functools.partial(strip_kernel, n, frames, cs, cf, taps_to...  82.5 us
    unnamed x13, local copies, waits for them, and re-layouts  4.35 us

profile of v1, /device:TPU:1, one launch (start us, length us, event | category | flops | bytes accessed | tf_op | source)
XLA Modules:
  0.0 92.8 jit_solution(3608250799159715373)
XLA Ops:
  0.6 0.0 copy-start.1
  0.6 0.0 copy-start.2
  0.7 0.0 copy-start
  0.7 0.0 copy-start.3
  0.7 1.0 %reduce-window.9 = s32[4,1]{0,1:T(1,128)S(1)} reduce-window(s32[4,1]{0,1:T(1,128)} %bitcast.27, s32[]{:T(128)} %constant.29.clone.1), window={size=4x1 pad=3_0x0_0}, to_apply=%region_0.0 | reduce-window | flops 12 | bytes 36 | tf_op jit(solution)/shard_map/reduce-window.4 | solution.py:697
  1.7 1.3 %fusion.4 = (s32[]{:T(128)}, s32[4]{0:T(128)S(1)}) fusion(s32[4]{0:T(128)} %param.10, s32[4,1]{0,1:T(1,128)S(1)} %reduce-window.9), kind=kLoop, calls=%fused_computation.24 | loop fusion | flops 7 | bytes 52 | tf_op jit(solution)/shard_map/reduce_sum | solution.py:606
  3.0 0.7 fusion.2
  3.6 0.1 and_convert_fusion
  3.7 0.7 add_select_fusion
  4.4 0.1 select_n.59
  4.5 0.1 le.34
  4.6 0.1 fusion.place
  4.7 0.8 copy.10
  5.5 0.6 gather_fusion
  6.0 0.1 broadcast_select_fusion
  6.1 0.1 le.31
  6.2 0.1 le.32
  6.3 0.1 broadcast_in_dim.49.bias
  6.4 0.1 broadcast_in_dim.50.keep
  6.5 1.0 %copy.18 = bf16[1,6,32,512]{3,1,2,0:T(8,128)(2,1)S(1)} copy(bf16[1,6,32,512]{3,2,1,0:T(8,128)(2,1)} %param.8) | data formatting | bytes 393216 | tf_op args[0]
  7.6 1.0 %copy.17 = bf16[1,6,32,512]{3,1,2,0:T(8,128)(2,1)S(1)} copy(bf16[1,6,32,512]{3,2,1,0:T(8,128)(2,1)} %param.9) | data formatting | bytes 393216 | tf_op args[1]
  8.7 0.0 copy-done.1
  8.7 0.0 copy-done.2
  8.7 0.0 copy-done
  8.7 0.0 copy-done.3
  8.7 82.5 %shard_map.95 = (bf16[32,8,512]{2,1,0:T(8,128)(2,1)S(1)}, bf16[32,8,512]{2,1,0:T(8,128)(2,1)S(1)}) custom-call(bf16[16,32]{1,0:T(8,128)(2,1)S(1)} %fusion.1.pick, bf16[32,16]{1,0:T(8,128)(2,1)S(1)} %fusion.place, f32[1,512]{1,0:T(1,128)S(1)} %bitcast.24, f32[4,16,1,128]{3,2,1,0:T(1,128)S(1)} %broadcast_in_dim.49.bias, ...), custom_call_target="tpu_custom_call" | custom-call | tf_op jit(solution)/shard_map/pallas_call | solution.py:649
  91.3 0.7 copy.13
  92.0 0.7 copy.14
  (10 shorter events, 0.2 us)
Async XLA Ops:
  0.6 8.1 %copy-start.1 = (bf16[4,128,512]{2,1,0:T(8,128)(2,1)S(1)}, bf16[4,128,512]{2,1,0:T(8,128)(2,1)}, u32[]{:S(2)}) copy-start(bf16[4,128,512]{2,1,0:T(8,128)(2,1)} %wa_in.1) | copy-start | bytes 1572868
  0.6 8.1 %copy-start.2 = (bf16[3,128,512]{2,1,0:T(8,128)(2,1)S(1)}, bf16[3,128,512]{2,1,0:T(8,128)(2,1)}, u32[]{:S(2)}) copy-start(bf16[3,128,512]{2,1,0:T(8,128)(2,1)} %wt_in.1) | copy-start | bytes 1179652
  0.7 8.1 %copy-start = (bf16[9,128,512]{2,1,0:T(8,128)(2,1)S(1)}, bf16[9,128,512]{2,1,0:T(8,128)(2,1)}, u32[]{:S(2)}) copy-start(bf16[9,128,512]{2,1,0:T(8,128)(2,1)} %ws_in.1) | copy-start | bytes 3538948
  0.7 8.1 %copy-start.3 = (f32[512]{0:T(512)S(1)}, f32[512]{0:T(512)}, u32[]{:S(2)}) copy-start(f32[512]{0:T(512)} %param.12) | copy-start | bytes 6148

commit v2 on v1

--- a/solution.py
+++ b/solution.py
@@ -201,12 +201,13 @@
 
 def strip_kernel(
     n, frames, cs, cf, taps_total,
-    pick, place, gain, bias, keep, clip_in, cot_in, ws_in, wt_in, wa_in,
+    rows_in, starts_in, gain, clip_in, cot_in, ws_in, wt_in, wa_in,
     out_block, out_grad,
     weights, clip_slab, cot_slab, clip_comp, cot_comp, clip_all, cot_all,
     shifted, pre, act_pad, resid, qs, ks, gs, att, gres, glow_pad, ghid,
     block_own, grad_own, block_z, grad_z, block_slab, grad_slab,
-    x_s, x_r, c0_s, c0_r, y_s, y_r, c1_s, c1_r, c2_s, c2_r, w_loc,
+    x_s, x_r, c0_s, c0_r, y_s, y_r, c1_s, c1_r, c2_s, c2_r,
+    z_s, z_r, yd_s, yd_r, zd_s, zd_r, c3_s, c3_r, c4_s, c4_r, w_loc,
     p1_s, p1_r, p1_l, p2_s, p2_r, p2_l, oz_s, oz_r, oz_l, ox_s, ox_r, ox_l,
 ):
     space = lax.axis_index("space")
@@ -230,6 +231,24 @@
             device_id=where, device_id_type=MESH_ID,
         )
 
+    bound = 0
+    bounds = []
+    for t in range(n):
+        bounds.append(bound)
+        bound = bound + rows_in[t]
+
+    def selection(shape, slot_dim):
+        slot = lax.broadcasted_iota(jnp.int32, shape, slot_dim)
+        row = lax.broadcasted_iota(jnp.int32, shape, 1 - slot_dim)
+        chosen = jnp.zeros(shape, WIDE)
+        for t in range(n):
+            offset = slot - t * SLOT_PAD
+            hit = (offset >= 0) & (offset < rows_in[t]) & (row == offset + bounds[t])
+            chosen = jnp.where(hit, 1.0, chosen)
+        return chosen.astype(LOW)
+
+    first_column = space * cs + frame * cf - 1
+
     barrier = pltpu.get_barrier_semaphore()
     for k in range(1, n):
         pl.semaphore_signal(barrier, inc=1, device_id={"space": (space + k) % n}, device_id_type=MESH_ID)
@@ -266,9 +285,24 @@
     my_rows = pl.ds(pl.multiple_of(group * half, half), half)
     other_rows = pl.ds(pl.multiple_of((1 - group) * half, half), half)
 
+    z_bit = frame % 2
+    peer = {"frame": frame + 1 - 2 * z_bit}
+    q_me = 2 * group + z_bit
+    q_y = 2 * (1 - group) + z_bit
+    q_z = 2 * group + 1 - z_bit
+    q_d = 2 * (1 - group) + 1 - z_bit
+    part = depth // 4
+
+    def quarter(q):
+        return pl.ds(pl.multiple_of(q * part, part), part)
+
+    def eighth(q, second):
+        return pl.ds(pl.multiple_of(q * part + second * (part // 2), part // 2), part // 2)
+
     def x_copy(m):
         ref, i = sources[m]
-        return remote(ref.at[i, my_rows], weights.at[m, space, my_rows], x_s.at[m], x_r.at[m], {"space": across})
+        rows = my_rows if m < taps_total else quarter(q_me)
+        return remote(ref.at[i, rows], weights.at[m, space, rows], x_s.at[m], x_r.at[m], {"space": across})
 
     def c0_copy(m):
         ref, i = sources[m]
@@ -317,6 +351,58 @@
         arrival(m, across_other, my_rows, c1_s, c1_r, {"space": partner}).wait_recv()
         arrival(m, across_other, other_rows, c2_s, c2_r, {"space": partner}).wait_recv()
 
+    flip = {"groups": 1 - group}
+    home = {"space": partner}
+
+    def quad_copy(m, rows, ssem, rsem, where):
+        piece = weights.at[m, across, rows]
+        return remote(piece, piece, ssem.at[m], rsem.at[m], where)
+
+    def quad_sends(m):
+        return (
+            quad_copy(m, quarter(q_me), y_s, y_r, flip),
+            quad_copy(m, quarter(q_me), z_s, z_r, peer),
+            quad_copy(m, quarter(q_me), c1_s, c1_r, home),
+            quad_copy(m, eighth(q_y, 0), zd_s, zd_r, peer),
+            quad_copy(m, quarter(q_y), c2_s, c2_r, home),
+            quad_copy(m, eighth(q_z, 1), yd_s, yd_r, flip),
+            quad_copy(m, quarter(q_z), c3_s, c3_r, home),
+            quad_copy(m, quarter(q_d), c4_s, c4_r, home),
+        )
+
+    def quad_first(m):
+        arrival(m, across, quarter(q_me), x_s, x_r, {"space": across}).wait_recv()
+        for copy in quad_sends(m)[0:3]:
+            copy.start()
+
+    def quad_second(m):
+        arrival(m, across, quarter(q_y), y_s, y_r, flip).wait_recv()
+        for copy in quad_sends(m)[3:5]:
+            copy.start()
+        arrival(m, across, quarter(q_z), z_s, z_r, peer).wait_recv()
+        for copy in quad_sends(m)[5:7]:
+            copy.start()
+
+    def quad_third(m):
+        arrival(m, across, eighth(q_d, 0), zd_s, zd_r, peer).wait_recv()
+        arrival(m, across, eighth(q_d, 1), yd_s, yd_r, flip).wait_recv()
+        quad_sends(m)[7].start()
+
+    def quad_ready(m):
+        arrival(m, partner, None, c0_s, c0_r, home).wait_recv()
+        arrival(m, across_other, quarter(q_me), c1_s, c1_r, home).wait_recv()
+        arrival(m, across_other, quarter(q_y), c2_s, c2_r, home).wait_recv()
+        arrival(m, across_other, quarter(q_z), c3_s, c3_r, home).wait_recv()
+        arrival(m, across_other, quarter(q_d), c4_s, c4_r, home).wait_recv()
+
+    reached = [taps_total, taps_total, taps_total, taps_total]
+
+    def advance(m):
+        for step, ahead, act in ((0, 2, quad_first), (1, 1, quad_second), (2, 0, quad_third), (3, 0, quad_ready)):
+            while reached[step] <= min(m + ahead, total - 1):
+                act(reached[step])
+                reached[step] += 1
+
     def compact(which):
         slab, comp = ((clip_slab, clip_comp), (cot_slab, cot_comp))[which]
         for k in range(1, n):
@@ -326,7 +412,7 @@
         @pl.loop(0, slab.shape[0])
         def _(col):
             rows = jnp.concatenate([slab[col, t].astype(WIDE) for t in range(n)], 0).astype(LOW)
-            comp[col] = dot_plain(pick[...], rows).astype(LOW)
+            comp[col] = dot_plain(pick, rows).astype(LOW)
 
     def p2_copy(which, k):
         comp, whole, grow = ((clip_comp, clip_all, 4), (cot_comp, cot_all, 2))[which]
@@ -345,6 +431,7 @@
         comp, whole, grow = ((clip_comp, clip_all, 4), (cot_comp, cot_all, 2))[which]
         return pltpu.make_async_copy(comp.at[pl.ds(cf * frame, cf + grow)], whole.at[:, frame], p2_l.at[which])
 
+    pick = selection((ROW_PAD, n * SLOT_PAD), 1)
     for which in range(2):
         compact(which)
         for k in range(1, frames):
@@ -375,18 +462,20 @@
 
     relay_first(0)
 
-    @pl.loop(0, taps_total)
-    def _(m):
-        relay_first(m + 1)
+    def tap(m):
         relay_second(m)
         ready(m)
         lhs = shifted[m // 3, pl.ds(m % 3, wide)].reshape(wide * full, channels)
         pre[...] += dot_plain(lhs, weight(m))
 
-    for m in range(taps_total + 1, total):
-        relay_first(m)
-    for m in range(taps_total, total):
-        relay_second(m)
+    @pl.loop(0, taps_total - 1)
+    def _(m):
+        relay_first(m + 1)
+        tap(m)
+
+    quad_first(taps_total)
+    reached[0] += 1
+    tap(taps_total - 1)
 
     @pl.loop(0, wide)
     def _(col):
@@ -396,24 +485,24 @@
     for k in range(1, frames):
         p2_arrival(1, k).wait_recv()
     p2_local(1).wait()
-    for m in range(taps_total, total):
-        ready(m)
 
     def flat(ref, lo, count):
         return ref[pl.ds(lo, count)].reshape(count * full, channels)
 
     mixed = flat(clip_all, 1, wide).astype(WIDE)
     for k in range(wt_in.shape[0]):
+        advance(first_temporal + k)
         mixed += dot_plain(
             act_pad[:, pl.ds(2 - k, frames)].reshape(wide * full, channels), weight(first_temporal + k)
         )
     low = mixed.astype(LOW)
     resid[...] = low.reshape(resid.shape)
 
-    @pl.loop(0, 3)
-    def _(i):
+    for i in range(3):
+        advance(first_attn + i)
         qs[i] = dot_plain(flat(resid, 0, wide), weight(first_attn + i)).astype(LOW).reshape(resid.shape)
 
+    advance(first_attn + 3)
     gs[...] = dot_back(flat(cot_all, 0, wide), weight(first_attn + 3)).astype(LOW).reshape(resid.shape)
 
     @pl.loop(0, wide)
@@ -424,9 +513,11 @@
         up = [gs[col, f].astype(WIDE) for f in range(frames)]
         gk = [None] * frames
         gv = [None] * frames
+        column = jnp.clip(first_column + col, 0, cs * n - 1)
         for f in range(frames):
+            start = starts_in[f, column]
             sc = [
-                jnp.sum(q[f] * kk[g], -1, keepdims=True) * scale + bias[col, f * frames + g][:, :1]
+                jnp.sum(q[f] * kk[g], -1, keepdims=True) * scale + jnp.where(start <= g, 0.0, -1e30)
                 for g in range(f + 1)
             ]
             top = sc[0]
@@ -510,7 +601,7 @@
         @pl.loop(0, frames)
         def _(f):
             for c in range(cf):
-                rows = dot_plain(place[...], z[f, c])
+                rows = dot_plain(place, z[f, c])
                 for t in range(n):
                     slab[t, f * cf + c] = rows[t * SLOT_PAD : (t + 1) * SLOT_PAD].astype(LOW)
 
@@ -518,6 +609,7 @@
             ox_copy(which, k).start()
         ox_local(which).start()
 
+    place = selection((n * SLOT_PAD, ROW_PAD), 0)
     send_frames(0)
     gres[...] = flat(cot_all, 0, wide).astype(WIDE)
 
@@ -537,7 +629,10 @@
 
     @pl.loop(0, wide)
     def _(col):
-        p = jnp.where(keep[col][:, :1] > 0.5, pre[pl.ds(col * full, full)], 0.0)
+        inside = (first_column + col >= 0) & (first_column + col < cs * n)
+        limit = jnp.where(inside, bound, 0)
+        row = lax.broadcasted_iota(jnp.int32, (full, channels), 0) % ROW_PAD
+        p = jnp.where(row < limit, pre[pl.ds(col * full, full)], 0.0)
         shifted[0, col] = pltpu.roll(p, 1, 0).astype(LOW)
         shifted[1, col] = p.astype(LOW)
         shifted[2, col] = pltpu.roll(p, full - 1, 0).astype(LOW)
@@ -573,9 +668,13 @@
     for m in range(total):
         x_copy(m).wait_send()
         c0_copy(m).wait_send()
-        y_copy(m).wait_send()
-        c1_copy(m).wait_send()
-        c2_copy(m).wait_send()
+        if m < taps_total:
+            y_copy(m).wait_send()
+            c1_copy(m).wait_send()
+            c2_copy(m).wait_send()
+        else:
+            for copy in quad_sends(m):
+                copy.wait_send()
 
 
 def per_device_strips(clip, cotangent, tile_rows, frame_start, norm_gain, w_spatial, w_temporal, w_attn):
@@ -584,8 +683,6 @@
     channels = clip.shape[3]
     n = lax.axis_size("space")
     frames = lax.axis_size("frame")
-    space = lax.axis_index("space")
-    frame = lax.axis_index("frame")
     cs = breadth // n
     cf = cs // frames
     wide = cf + 2
@@ -593,25 +690,12 @@
     depth = w_spatial.shape[1]
     taps_total = w_spatial.shape[0]
     total = taps_total + w_temporal.shape[0] + w_attn.shape[0]
-    bounds = jnp.cumsum(tile_rows) - tile_rows
-    slot_ids = jnp.arange(SLOT_PAD)
-    row_of = jnp.where(slot_ids[None, :] < tile_rows[:, None], bounds[:, None] + slot_ids[None, :], -1).reshape(-1)
-    place = (row_of[:, None] == jnp.arange(ROW_PAD)[None, :]).astype(LOW)
-    pick = (row_of[None, :] == jnp.arange(ROW_PAD)[:, None]).astype(LOW)
-    columns = space * cs + frame * cf - 1 + jnp.arange(wide)
-    inside = (columns >= 0) & (columns < breadth)
-    starts = jnp.take(frame_start, jnp.clip(columns, 0, breadth - 1), axis=1)
-    bias = jnp.where(starts.T[:, :, None] <= jnp.arange(frames)[None, None, :], 0.0, -1e30).astype(WIDE)
-    bias = jnp.broadcast_to(bias.reshape(wide, frames * frames, 1, 1), (wide, frames * frames, 1, 128))
-    live_row = (jnp.arange(full) % ROW_PAD) < jnp.sum(tile_rows)
-    keep = jnp.broadcast_to(
-        (inside[:, None] & live_row[None, :]).astype(WIDE)[:, :, None], (wide, full, 128)
-    )
     def by_column(values, halo):
         turned = jnp.transpose(values[0], (1, 0, 2))
         return jnp.pad(turned, ((halo, halo), (0, SLOT_PAD - slots), (0, 0)))
 
     vmem = pl.BlockSpec(memory_space=pltpu.VMEM)
+    smem = pl.BlockSpec(memory_space=pltpu.SMEM)
     hbm = pl.BlockSpec(memory_space=pl.ANY)
     dma = pltpu.SemaphoreType.DMA
     shape4 = (frames, ROW_PAD, channels)
@@ -641,7 +725,7 @@
         pltpu.VMEM((n, cs, SLOT_PAD, channels), LOW),
         pltpu.VMEM((n, cs, SLOT_PAD, channels), LOW),
     ]
-    scratch += [dma((total,)) for _ in range(11)]
+    scratch += [dma((total,)) for _ in range(21)]
     scratch += [dma((2, n - 1)), dma((2, n - 1)), dma((2,))]
     scratch += [dma((2, frames - 1)), dma((2, frames - 1)), dma((2,))] * 2
     scratch += [dma((2, n - 1)), dma((2, n - 1)), dma((2,))]
@@ -649,14 +733,14 @@
     block, grad = pl.pallas_call(
         functools.partial(strip_kernel, n, frames, cs, cf, taps_total),
         out_shape=(out, out),
-        in_specs=[vmem] * 5 + [hbm] * 5,
+        in_specs=[smem] * 2 + [vmem] + [hbm] * 5,
         out_specs=(vmem, vmem),
         scratch_shapes=scratch,
         compiler_params=pltpu.CompilerParams(
             collective_id=0, has_side_effects=True, vmem_limit_bytes=48 * 1024 * 1024
         ),
     )(
-        pick, place, norm_gain.reshape(1, channels), bias, keep,
+        tile_rows, frame_start, norm_gain.reshape(1, channels),
         by_column(clip, 2), by_column(cotangent, 1), w_spatial, w_temporal, w_attn,
     )
 
@@ -677,6 +761,7 @@
         and slots_all // n <= SLOT_PAD
         and slots_all // 2 < ROW_PAD
         and channels % (128 * n) == 0
+        and frames % 2 == 0
     )
 
 

time: 93 us -> 95.3 us (1.025)
  Pallas kernels: 82.5 us -> 89.3 us
  other arithmetic: 3.9 us -> 0 us
    pallas_call x1, Pallas kernels: 82.5 us -> 89.3 us  [per_device_strips(): pl.pallas_call(functools.partial(strip_kernel, n, frames, cs, cf, taps_to...]
    reduce_sum x1 -> x0, other arithmetic: 1.29 us -> none  [per_device_strips(): live_row = jnp.arange(full) % ROW_PAD < jnp.sum(tile_rows)]
    another operation x1 -> x0, other arithmetic: 0.97 us -> none  [run(): jax.shard_map(per_device_strips if fits else per_device, mesh=mesh, in_sp...]
    unnamed x13 -> x16, local copies, waits for them, and re-layouts: 4.35 us -> 4.69 us
where the time goes in v2:
time: 95.3 us; the launch traced here: 94.8 us
  Pallas kernels  89.3 us (94%)
  local copies, waits for them, and re-layouts  4.82 us (5%)
    pallas_call x1, Pallas kernels, per_device_strips(): pl.pallas_call(functools.partial(strip_kernel, n, frames, cs, cf, taps_to...  89.3 us
    unnamed x16, local copies, waits for them, and re-layouts  4.69 us

profile of v2, /device:TPU:1, one launch (start us, length us, event | category | flops | bytes accessed | tf_op | source)
XLA Modules:
  0.0 94.8 jit_solution(11043308767618888402)
XLA Ops:
  0.6 0.0 copy-start.1
  0.6 0.0 copy-start
  0.7 0.0 copy-start.4
  0.7 0.0 copy-start.3
  0.7 0.0 copy-start.5
  0.7 1.2 %copy.17 = bf16[1,6,32,512]{3,1,2,0:T(8,128)(2,1)S(1)} copy(bf16[1,6,32,512]{3,2,1,0:T(8,128)(2,1)} %param.8) | data formatting | bytes 393216 | tf_op args[0]
  1.9 1.0 %copy.16 = bf16[1,6,32,512]{3,1,2,0:T(8,128)(2,1)S(1)} copy(bf16[1,6,32,512]{3,2,1,0:T(8,128)(2,1)} %param.9) | data formatting | bytes 393216 | tf_op args[1]
  3.0 0.0 copy-done.1
  3.0 0.0 copy-done
  3.0 0.0 copy-done.4
  3.0 0.0 copy-done.3
  3.0 0.0 copy-done.5
  3.0 0.0 copy-start.2
  3.1 1.0 %copy-done.2 = bf16[3,128,512]{2,1,0:T(8,128)(2,1)S(1)} copy-done((bf16[3,128,512]{2,1,0:T(8,128)(2,1)S(1)}, bf16[3,128,512]{2,1,0:T(8,128)(2,1)}, u32[]{:S(2)}) %copy-start.2) | copy-done | bytes 393240
  4.0 89.3 %shard_map.95 = (bf16[32,8,512]{2,1,0:T(8,128)(2,1)S(1)}, bf16[32,8,512]{2,1,0:T(8,128)(2,1)S(1)}) custom-call(s32[4]{0:T(128)S(1)} %copy-done.5, s32[4,32]{1,0:T(4,128)S(1)} %copy-done.3, f32[1,512]{1,0:T(1,128)S(1)} %bitcast.19, bf16[36,8,512]{2,1,0:T(8,128)(2,1)S(1)} %pad.8.clip_in, bf16[34,8,512]{2,1,0:T(8,128)(2,1)S(1)} %pad.9.cot_in, ...), custom_call_target="tpu_custom_call" | custom-call | tf_op jit(solution)/shard_map/pallas_call | solution.py:733
  93.4 0.7 copy.13
  94.1 0.7 copy.12
  (3 shorter events, 0.1 us)
Async XLA Ops:
  0.6 2.4 %copy-start.1 = (bf16[4,128,512]{2,1,0:T(8,128)(2,1)S(1)}, bf16[4,128,512]{2,1,0:T(8,128)(2,1)}, u32[]{:S(2)}) copy-start(bf16[4,128,512]{2,1,0:T(8,128)(2,1)} %wa_in.1) | copy-start | bytes 1572868
  0.6 2.4 %copy-start = (bf16[9,128,512]{2,1,0:T(8,128)(2,1)S(1)}, bf16[9,128,512]{2,1,0:T(8,128)(2,1)}, u32[]{:S(2)}) copy-start(bf16[9,128,512]{2,1,0:T(8,128)(2,1)} %ws_in.1) | copy-start | bytes 3538948
  0.7 2.4 %copy-start.4 = (f32[512]{0:T(512)S(1)}, f32[512]{0:T(512)}, u32[]{:S(2)}) copy-start(f32[512]{0:T(512)} %param.12) | copy-start | bytes 6148
  0.7 2.4 %copy-start.3 = (s32[4,32]{1,0:T(4,128)S(1)}, s32[4,32]{1,0:T(4,128)}, u32[]{:S(2)}) copy-start(s32[4,32]{1,0:T(4,128)} %starts_in.1) | copy-start | bytes 1540
  0.7 2.4 %copy-start.5 = (s32[4]{0:T(128)S(1)}, s32[4]{0:T(128)}, u32[]{:S(2)}) copy-start(s32[4]{0:T(128)} %rows_in.1) | copy-start | bytes 52
  3.0 1.0 %copy-start.2 = (bf16[3,128,512]{2,1,0:T(8,128)(2,1)S(1)}, bf16[3,128,512]{2,1,0:T(8,128)(2,1)}, u32[]{:S(2)}) copy-start(bf16[3,128,512]{2,1,0:T(8,128)(2,1)} %wt_in.1) | copy-start | bytes 1179652

commit v3 on v1

--- a/solution.py
+++ b/solution.py
@@ -188,6 +188,7 @@
 LOW = jnp.bfloat16
 WIDE = jnp.float32
 ROW_PAD = 16
+LAG = 3
 SLOT_PAD = 8
 
 
@@ -201,7 +202,7 @@
 
 def strip_kernel(
     n, frames, cs, cf, taps_total,
-    pick, place, gain, bias, keep, clip_in, cot_in, ws_in, wt_in, wa_in,
+    rows_in, starts_in, gain, clip_in, cot_in, ws_in, wt_in, wa_in,
     out_block, out_grad,
     weights, clip_slab, cot_slab, clip_comp, cot_comp, clip_all, cot_all,
     shifted, pre, act_pad, resid, qs, ks, gs, att, gres, glow_pad, ghid,
@@ -230,6 +231,24 @@
             device_id=where, device_id_type=MESH_ID,
         )
 
+    bound = 0
+    bounds = []
+    for t in range(n):
+        bounds.append(bound)
+        bound = bound + rows_in[t]
+
+    def selection(shape, slot_dim):
+        slot = lax.broadcasted_iota(jnp.int32, shape, slot_dim)
+        row = lax.broadcasted_iota(jnp.int32, shape, 1 - slot_dim)
+        chosen = jnp.zeros(shape, WIDE)
+        for t in range(n):
+            offset = slot - t * SLOT_PAD
+            hit = (offset >= 0) & (offset < rows_in[t]) & (row == offset + bounds[t])
+            chosen = jnp.where(hit, 1.0, chosen)
+        return chosen.astype(LOW)
+
+    first_column = space * cs + frame * cf - 1
+
     barrier = pltpu.get_barrier_semaphore()
     for k in range(1, n):
         pl.semaphore_signal(barrier, inc=1, device_id={"space": (space + k) % n}, device_id_type=MESH_ID)
@@ -326,7 +345,7 @@
         @pl.loop(0, slab.shape[0])
         def _(col):
             rows = jnp.concatenate([slab[col, t].astype(WIDE) for t in range(n)], 0).astype(LOW)
-            comp[col] = dot_plain(pick[...], rows).astype(LOW)
+            comp[col] = dot_plain(pick, rows).astype(LOW)
 
     def p2_copy(which, k):
         comp, whole, grow = ((clip_comp, clip_all, 4), (cot_comp, cot_all, 2))[which]
@@ -345,6 +364,7 @@
         comp, whole, grow = ((clip_comp, clip_all, 4), (cot_comp, cot_all, 2))[which]
         return pltpu.make_async_copy(comp.at[pl.ds(cf * frame, cf + grow)], whole.at[:, frame], p2_l.at[which])
 
+    pick = selection((ROW_PAD, n * SLOT_PAD), 1)
     for which in range(2):
         compact(which)
         for k in range(1, frames):
@@ -353,6 +373,12 @@
 
     act_pad[:, 0:2] = jnp.zeros((wide, 2, ROW_PAD, channels), LOW)
     glow_pad[:, frames : frames + 2] = jnp.zeros((wide, 2, ROW_PAD, channels), LOW)
+    ahead = total - taps_total
+    behind = ahead - LAG
+    for m in range(ahead):
+        relay_first(m)
+        if m >= LAG:
+            relay_second(m - LAG)
     for k in range(1, frames):
         p2_arrival(0, k).wait_recv()
     p2_local(0).wait()
@@ -373,19 +399,15 @@
     def weight(m):
         return weights[m].reshape(n * depth, channels)
 
-    relay_first(0)
-
     @pl.loop(0, taps_total)
     def _(m):
-        relay_first(m + 1)
-        relay_second(m)
+        relay_first(m + ahead)
+        relay_second(m + behind)
         ready(m)
         lhs = shifted[m // 3, pl.ds(m % 3, wide)].reshape(wide * full, channels)
         pre[...] += dot_plain(lhs, weight(m))
 
-    for m in range(taps_total + 1, total):
-        relay_first(m)
-    for m in range(taps_total, total):
+    for m in range(taps_total + behind, total):
         relay_second(m)
 
     @pl.loop(0, wide)
@@ -396,24 +418,24 @@
     for k in range(1, frames):
         p2_arrival(1, k).wait_recv()
     p2_local(1).wait()
-    for m in range(taps_total, total):
-        ready(m)
 
     def flat(ref, lo, count):
         return ref[pl.ds(lo, count)].reshape(count * full, channels)
 
     mixed = flat(clip_all, 1, wide).astype(WIDE)
     for k in range(wt_in.shape[0]):
+        ready(first_temporal + k)
         mixed += dot_plain(
             act_pad[:, pl.ds(2 - k, frames)].reshape(wide * full, channels), weight(first_temporal + k)
         )
     low = mixed.astype(LOW)
     resid[...] = low.reshape(resid.shape)
 
-    @pl.loop(0, 3)
-    def _(i):
+    for i in range(3):
+        ready(first_attn + i)
         qs[i] = dot_plain(flat(resid, 0, wide), weight(first_attn + i)).astype(LOW).reshape(resid.shape)
 
+    ready(first_attn + 3)
     gs[...] = dot_back(flat(cot_all, 0, wide), weight(first_attn + 3)).astype(LOW).reshape(resid.shape)
 
     @pl.loop(0, wide)
@@ -424,9 +446,11 @@
         up = [gs[col, f].astype(WIDE) for f in range(frames)]
         gk = [None] * frames
         gv = [None] * frames
+        column = jnp.clip(first_column + col, 0, cs * n - 1)
         for f in range(frames):
+            start = starts_in[f, column]
             sc = [
-                jnp.sum(q[f] * kk[g], -1, keepdims=True) * scale + bias[col, f * frames + g][:, :1]
+                jnp.sum(q[f] * kk[g], -1, keepdims=True) * scale + jnp.where(start <= g, 0.0, -1e30)
                 for g in range(f + 1)
             ]
             top = sc[0]
@@ -510,7 +534,7 @@
         @pl.loop(0, frames)
         def _(f):
             for c in range(cf):
-                rows = dot_plain(place[...], z[f, c])
+                rows = dot_plain(place, z[f, c])
                 for t in range(n):
                     slab[t, f * cf + c] = rows[t * SLOT_PAD : (t + 1) * SLOT_PAD].astype(LOW)
 
@@ -518,6 +542,7 @@
             ox_copy(which, k).start()
         ox_local(which).start()
 
+    place = selection((n * SLOT_PAD, ROW_PAD), 0)
     send_frames(0)
     gres[...] = flat(cot_all, 0, wide).astype(WIDE)
 
@@ -537,7 +562,10 @@
 
     @pl.loop(0, wide)
     def _(col):
-        p = jnp.where(keep[col][:, :1] > 0.5, pre[pl.ds(col * full, full)], 0.0)
+        inside = (first_column + col >= 0) & (first_column + col < cs * n)
+        limit = jnp.where(inside, bound, 0)
+        row = lax.broadcasted_iota(jnp.int32, (full, channels), 0) % ROW_PAD
+        p = jnp.where(row < limit, pre[pl.ds(col * full, full)], 0.0)
         shifted[0, col] = pltpu.roll(p, 1, 0).astype(LOW)
         shifted[1, col] = p.astype(LOW)
         shifted[2, col] = pltpu.roll(p, full - 1, 0).astype(LOW)
@@ -584,8 +612,6 @@
     channels = clip.shape[3]
     n = lax.axis_size("space")
     frames = lax.axis_size("frame")
-    space = lax.axis_index("space")
-    frame = lax.axis_index("frame")
     cs = breadth // n
     cf = cs // frames
     wide = cf + 2
@@ -593,25 +619,12 @@
     depth = w_spatial.shape[1]
     taps_total = w_spatial.shape[0]
     total = taps_total + w_temporal.shape[0] + w_attn.shape[0]
-    bounds = jnp.cumsum(tile_rows) - tile_rows
-    slot_ids = jnp.arange(SLOT_PAD)
-    row_of = jnp.where(slot_ids[None, :] < tile_rows[:, None], bounds[:, None] + slot_ids[None, :], -1).reshape(-1)
-    place = (row_of[:, None] == jnp.arange(ROW_PAD)[None, :]).astype(LOW)
-    pick = (row_of[None, :] == jnp.arange(ROW_PAD)[:, None]).astype(LOW)
-    columns = space * cs + frame * cf - 1 + jnp.arange(wide)
-    inside = (columns >= 0) & (columns < breadth)
-    starts = jnp.take(frame_start, jnp.clip(columns, 0, breadth - 1), axis=1)
-    bias = jnp.where(starts.T[:, :, None] <= jnp.arange(frames)[None, None, :], 0.0, -1e30).astype(WIDE)
-    bias = jnp.broadcast_to(bias.reshape(wide, frames * frames, 1, 1), (wide, frames * frames, 1, 128))
-    live_row = (jnp.arange(full) % ROW_PAD) < jnp.sum(tile_rows)
-    keep = jnp.broadcast_to(
-        (inside[:, None] & live_row[None, :]).astype(WIDE)[:, :, None], (wide, full, 128)
-    )
     def by_column(values, halo):
         turned = jnp.transpose(values[0], (1, 0, 2))
         return jnp.pad(turned, ((halo, halo), (0, SLOT_PAD - slots), (0, 0)))
 
     vmem = pl.BlockSpec(memory_space=pltpu.VMEM)
+    smem = pl.BlockSpec(memory_space=pltpu.SMEM)
     hbm = pl.BlockSpec(memory_space=pl.ANY)
     dma = pltpu.SemaphoreType.DMA
     shape4 = (frames, ROW_PAD, channels)
@@ -649,14 +662,14 @@
     block, grad = pl.pallas_call(
         functools.partial(strip_kernel, n, frames, cs, cf, taps_total),
         out_shape=(out, out),
-        in_specs=[vmem] * 5 + [hbm] * 5,
+        in_specs=[smem] * 2 + [vmem] + [hbm] * 5,
         out_specs=(vmem, vmem),
         scratch_shapes=scratch,
         compiler_params=pltpu.CompilerParams(
             collective_id=0, has_side_effects=True, vmem_limit_bytes=48 * 1024 * 1024
         ),
     )(
-        pick, place, norm_gain.reshape(1, channels), bias, keep,
+        tile_rows, frame_start, norm_gain.reshape(1, channels),
         by_column(clip, 2), by_column(cotangent, 1), w_spatial, w_temporal, w_attn,
     )
 

time: 93 us -> 70.3 us (0.76)
  Pallas kernels: 82.5 us -> 64.6 us
  other arithmetic: 3.9 us -> 0 us
    pallas_call x1, Pallas kernels: 82.5 us -> 64.6 us  [per_device_strips(): pl.pallas_call(functools.partial(strip_kernel, n, frames, cs, cf, taps_to...]
    reduce_sum x1 -> x0, other arithmetic: 1.29 us -> none  [per_device_strips(): live_row = jnp.arange(full) % ROW_PAD < jnp.sum(tile_rows)]
    another operation x1 -> x0, other arithmetic: 0.97 us -> none  [run(): jax.shard_map(per_device_strips if fits else per_device, mesh=mesh, in_sp...]
    unnamed x13 -> x16, local copies, waits for them, and re-layouts: 4.35 us -> 4.69 us
where the time goes in v3:
time: 70.3 us; the launch traced here: 70.1 us
  Pallas kernels  64.6 us (92%)
  local copies, waits for them, and re-layouts  4.82 us (7%)
  between operations  0.76 us (1%)
    pallas_call x1, Pallas kernels, per_device_strips(): pl.pallas_call(functools.partial(strip_kernel, n, frames, cs, cf, taps_to...  64.6 us
    unnamed x16, local copies, waits for them, and re-layouts  4.69 us

profile of v3, /device:TPU:1, one launch (start us, length us, event | category | flops | bytes accessed | tf_op | source)
XLA Modules:
  0.0 70.1 jit_solution(13762927423549132849)
XLA Ops:
  0.6 0.0 copy-start.1
  0.6 0.0 copy-start
  0.7 0.0 copy-start.4
  0.7 0.0 copy-start.3
  0.7 0.0 copy-start.5
  0.7 1.2 %copy.17 = bf16[1,6,32,512]{3,1,2,0:T(8,128)(2,1)S(1)} copy(bf16[1,6,32,512]{3,2,1,0:T(8,128)(2,1)} %param.8) | data formatting | bytes 393216 | tf_op args[0]
  1.9 1.0 %copy.16 = bf16[1,6,32,512]{3,1,2,0:T(8,128)(2,1)S(1)} copy(bf16[1,6,32,512]{3,2,1,0:T(8,128)(2,1)} %param.9) | data formatting | bytes 393216 | tf_op args[1]
  3.0 0.0 copy-done.1
  3.0 0.0 copy-done
  3.0 0.0 copy-done.4
  3.0 0.0 copy-done.3
  3.0 0.0 copy-done.5
  3.0 0.0 copy-start.2
  3.1 1.0 %copy-done.2 = bf16[3,128,512]{2,1,0:T(8,128)(2,1)S(1)} copy-done((bf16[3,128,512]{2,1,0:T(8,128)(2,1)S(1)}, bf16[3,128,512]{2,1,0:T(8,128)(2,1)}, u32[]{:S(2)}) %copy-start.2) | copy-done | bytes 393240
  4.0 64.6 %shard_map.95 = (bf16[32,8,512]{2,1,0:T(8,128)(2,1)S(1)}, bf16[32,8,512]{2,1,0:T(8,128)(2,1)S(1)}) custom-call(s32[4]{0:T(128)S(1)} %copy-done.5, s32[4,32]{1,0:T(4,128)S(1)} %copy-done.3, f32[1,512]{1,0:T(1,128)S(1)} %bitcast.19, bf16[36,8,512]{2,1,0:T(8,128)(2,1)S(1)} %pad.8.clip_in, bf16[34,8,512]{2,1,0:T(8,128)(2,1)S(1)} %pad.9.cot_in, ...), custom_call_target="tpu_custom_call" | custom-call | tf_op jit(solution)/shard_map/pallas_call | solution.py:662
  68.7 0.7 %copy.13 = bf16[1,6,32,512]{3,2,1,0:T(8,128)(2,1)} copy(bf16[1,6,32,512]{3,1,2,0:T(8,128)(2,1)S(1)} %get-tuple-element.8) | data formatting | bytes 393216
  69.4 0.7 %copy.12 = bf16[1,6,32,512]{3,2,1,0:T(8,128)(2,1)} copy(bf16[1,6,32,512]{3,1,2,0:T(8,128)(2,1)S(1)} %get-tuple-element.9) | data formatting | bytes 393216
  (3 shorter events, 0.1 us)
Async XLA Ops:
  0.6 2.4 %copy-start.1 = (bf16[4,128,512]{2,1,0:T(8,128)(2,1)S(1)}, bf16[4,128,512]{2,1,0:T(8,128)(2,1)}, u32[]{:S(2)}) copy-start(bf16[4,128,512]{2,1,0:T(8,128)(2,1)} %wa_in.1) | copy-start | bytes 1572868
  0.6 2.4 %copy-start = (bf16[9,128,512]{2,1,0:T(8,128)(2,1)S(1)}, bf16[9,128,512]{2,1,0:T(8,128)(2,1)}, u32[]{:S(2)}) copy-start(bf16[9,128,512]{2,1,0:T(8,128)(2,1)} %ws_in.1) | copy-start | bytes 3538948
  0.7 2.4 %copy-start.4 = (f32[512]{0:T(512)S(1)}, f32[512]{0:T(512)}, u32[]{:S(2)}) copy-start(f32[512]{0:T(512)} %param.12) | copy-start | bytes 6148
  0.7 2.4 %copy-start.3 = (s32[4,32]{1,0:T(4,128)S(1)}, s32[4,32]{1,0:T(4,128)}, u32[]{:S(2)}) copy-start(s32[4,32]{1,0:T(4,128)} %starts_in.1) | copy-start | bytes 1540
  0.7 2.4 %copy-start.5 = (s32[4]{0:T(128)S(1)}, s32[4]{0:T(128)}, u32[]{:S(2)}) copy-start(s32[4]{0:T(128)} %rows_in.1) | copy-start | bytes 52
  3.0 1.0 %copy-start.2 = (bf16[3,128,512]{2,1,0:T(8,128)(2,1)S(1)}, bf16[3,128,512]{2,1,0:T(8,128)(2,1)}, u32[]{:S(2)}) copy-start(bf16[3,128,512]{2,1,0:T(8,128)(2,1)} %wt_in.1) | copy-start | bytes 1179652

commit v4 on v3

--- a/solution.py
+++ b/solution.py
@@ -342,7 +342,7 @@
             p1_arrival(which, k).wait_recv()
         p1_local(which).wait()
 
-        @pl.loop(0, slab.shape[0])
+        @pl.loop(0, slab.shape[0], unroll=True)
         def _(col):
             rows = jnp.concatenate([slab[col, t].astype(WIDE) for t in range(n)], 0).astype(LOW)
             comp[col] = dot_plain(pick, rows).astype(LOW)
@@ -383,7 +383,7 @@
         p2_arrival(0, k).wait_recv()
     p2_local(0).wait()
 
-    @pl.loop(0, wide + 2)
+    @pl.loop(0, wide + 2, unroll=2)
     def _(col):
         x = clip_all[col].reshape(full, channels).astype(WIDE)
         inverse = lax.rsqrt(jnp.mean(x * x, -1, keepdims=True) + NORM_EPSILON)
@@ -531,7 +531,7 @@
             oz_arrival(which, k).wait_recv()
         oz_local(which).wait()
 
-        @pl.loop(0, frames)
+        @pl.loop(0, frames, unroll=True)
         def _(f):
             for c in range(cf):
                 rows = dot_plain(place, z[f, c])
@@ -544,11 +544,10 @@
 
     place = selection((n * SLOT_PAD, ROW_PAD), 0)
     send_frames(0)
-    gres[...] = flat(cot_all, 0, wide).astype(WIDE)
-
-    @pl.loop(0, 3)
-    def _(i):
-        gres[...] += dot_back(flat(ks.at[i], 0, wide), weight(first_attn + i))
+    grad_sum = flat(cot_all, 0, wide).astype(WIDE)
+    for i in range(3):
+        grad_sum += dot_back(flat(ks.at[i], 0, wide), weight(first_attn + i))
+    gres[...] = grad_sum
 
     glow_pad[:, pl.ds(0, frames)] = gres[...].astype(LOW).reshape(resid.shape)
     send_tiles(0)
@@ -570,12 +569,12 @@
         shifted[1, col] = p.astype(LOW)
         shifted[2, col] = pltpu.roll(p, full - 1, 0).astype(LOW)
 
-    ghid[...] = jnp.zeros_like(ghid)
-
-    @pl.loop(0, taps_total)
-    def _(m):
+    total_back = None
+    for m in range(taps_total):
         lhs = shifted[2 - m // 3, pl.ds(2 - m % 3, cf)].reshape(cf * full, channels)
-        ghid[...] += dot_back(lhs, weight(m))
+        term = dot_back(lhs, weight(m))
+        total_back = term if total_back is None else total_back + term
+    ghid[...] = total_back
 
     for c in range(cf):
         x = clip_all[c + 2].reshape(full, channels).astype(WIDE)

time: 70.3 us -> 67.6 us (0.962)
  Pallas kernels: 64.6 us -> 61.9 us
    pallas_call x1, Pallas kernels: 64.6 us -> 61.9 us  [per_device_strips(): pl.pallas_call(functools.partial(strip_kernel, n, frames, cs, cf, taps_to...]
where the time goes in v4:
time: 67.6 us; the launch traced here: 67.4 us
  Pallas kernels  61.9 us (92%)
  local copies, waits for them, and re-layouts  4.82 us (7%)
  between operations  0.76 us (1%)
    pallas_call x1, Pallas kernels, per_device_strips(): pl.pallas_call(functools.partial(strip_kernel, n, frames, cs, cf, taps_to...  61.9 us
    unnamed x16, local copies, waits for them, and re-layouts  4.69 us

profile of v4, /device:TPU:1, one launch (start us, length us, event | category | flops | bytes accessed | tf_op | source)
XLA Modules:
  0.0 67.4 jit_solution(715941428859673376)
XLA Ops:
  0.6 0.0 copy-start.1
  0.6 0.0 copy-start
  0.7 0.0 copy-start.4
  0.7 0.0 copy-start.3
  0.7 0.0 copy-start.5
  0.7 1.2 %copy.17 = bf16[1,6,32,512]{3,1,2,0:T(8,128)(2,1)S(1)} copy(bf16[1,6,32,512]{3,2,1,0:T(8,128)(2,1)} %param.8) | data formatting | bytes 393216 | tf_op args[0]
  1.9 1.0 %copy.16 = bf16[1,6,32,512]{3,1,2,0:T(8,128)(2,1)S(1)} copy(bf16[1,6,32,512]{3,2,1,0:T(8,128)(2,1)} %param.9) | data formatting | bytes 393216 | tf_op args[1]
  3.0 0.0 copy-done.1
  3.0 0.0 copy-done
  3.0 0.0 copy-done.4
  3.0 0.0 copy-done.3
  3.0 0.0 copy-done.5
  3.0 0.0 copy-start.2
  3.1 1.0 %copy-done.2 = bf16[3,128,512]{2,1,0:T(8,128)(2,1)S(1)} copy-done((bf16[3,128,512]{2,1,0:T(8,128)(2,1)S(1)}, bf16[3,128,512]{2,1,0:T(8,128)(2,1)}, u32[]{:S(2)}) %copy-start.2) | copy-done | bytes 393240
  4.0 61.9 %shard_map.95 = (bf16[32,8,512]{2,1,0:T(8,128)(2,1)S(1)}, bf16[32,8,512]{2,1,0:T(8,128)(2,1)S(1)}) custom-call(s32[4]{0:T(128)S(1)} %copy-done.5, s32[4,32]{1,0:T(4,128)S(1)} %copy-done.3, f32[1,512]{1,0:T(1,128)S(1)} %bitcast.19, bf16[36,8,512]{2,1,0:T(8,128)(2,1)S(1)} %pad.8.clip_in, bf16[34,8,512]{2,1,0:T(8,128)(2,1)S(1)} %pad.9.cot_in, ...), custom_call_target="tpu_custom_call" | custom-call | tf_op jit(solution)/shard_map/pallas_call | solution.py:661
  66.0 0.7 %copy.13 = bf16[1,6,32,512]{3,2,1,0:T(8,128)(2,1)} copy(bf16[1,6,32,512]{3,1,2,0:T(8,128)(2,1)S(1)} %get-tuple-element.8) | data formatting | bytes 393216
  66.7 0.7 %copy.12 = bf16[1,6,32,512]{3,2,1,0:T(8,128)(2,1)} copy(bf16[1,6,32,512]{3,1,2,0:T(8,128)(2,1)S(1)} %get-tuple-element.9) | data formatting | bytes 393216
  (3 shorter events, 0.1 us)
Async XLA Ops:
  0.6 2.4 %copy-start.1 = (bf16[4,128,512]{2,1,0:T(8,128)(2,1)S(1)}, bf16[4,128,512]{2,1,0:T(8,128)(2,1)}, u32[]{:S(2)}) copy-start(bf16[4,128,512]{2,1,0:T(8,128)(2,1)} %wa_in.1) | copy-start | bytes 1572868
  0.6 2.4 %copy-start = (bf16[9,128,512]{2,1,0:T(8,128)(2,1)S(1)}, bf16[9,128,512]{2,1,0:T(8,128)(2,1)}, u32[]{:S(2)}) copy-start(bf16[9,128,512]{2,1,0:T(8,128)(2,1)} %ws_in.1) | copy-start | bytes 3538948
  0.7 2.4 %copy-start.4 = (f32[512]{0:T(512)S(1)}, f32[512]{0:T(512)}, u32[]{:S(2)}) copy-start(f32[512]{0:T(512)} %param.12) | copy-start | bytes 6148
  0.7 2.4 %copy-start.3 = (s32[4,32]{1,0:T(4,128)S(1)}, s32[4,32]{1,0:T(4,128)}, u32[]{:S(2)}) copy-start(s32[4,32]{1,0:T(4,128)} %starts_in.1) | copy-start | bytes 1540
  0.7 2.4 %copy-start.5 = (s32[4]{0:T(128)S(1)}, s32[4]{0:T(128)}, u32[]{:S(2)}) copy-start(s32[4]{0:T(128)} %rows_in.1) | copy-start | bytes 52
  3.0 1.0 %copy-start.2 = (bf16[3,128,512]{2,1,0:T(8,128)(2,1)S(1)}, bf16[3,128,512]{2,1,0:T(8,128)(2,1)}, u32[]{:S(2)}) copy-start(bf16[3,128,512]{2,1,0:T(8,128)(2,1)} %wt_in.1) | copy-start | bytes 1179652
